TPU v7x, 256 devices: a whole 4x4x8 slice. The times are simulated.
256 devices in a mesh: space: 16 (over x, z_hi), tm: 16 (over y, z_lo, core).
Axes of the slice: x: 4, y: 4, z: 8 (z_hi: 4, z_lo: 2; z = z_hi * 2 + z_lo), core: 2. Of those that a mesh axis runs over, the one named last changes fastest.
Arguments:
- latent: float32 [24, 1024, 2048], P(None, 'space', 'tm'), may hold values from -1.8 to 1.8
- events: int32 [24, 1024, 2048], P(None, 'space', 'tm'), may hold values from 0 to 7
- log_base: float32 [24, 1024, 2048], P(None, 'space', 'tm'), may hold values from -1.5 to 0.5
- innovation: float32 [24, 1024, 2048], P(None, 'space', 'tm'), may hold values from -6 to 6
- kappa_sq: float32 [24, 1024], replicated, may hold values from 0.3 to 3
- chol_factor: float32 [2048, 2048], P(None, 'tm'), as said below
- step_size: float32 [1], replicated, may hold values from 0.02 to 0.08
Outputs:
- gradient: float32 [24, 1024, 2048], P(None, 'space', 'tm')
- proposal: float32 [24, 1024, 2048], P(None, 'space', 'tm')
Inputs may be any that keep to these rules, and one draw needn't show every extreme that they name: chol_factor is lower triangular with a positive diagonal.
All inputs are finite; a program needn't handle non-finite values.
Results may differ from a plain program's by a relative error of at most 0.000067.
Values sent between devices are 32-bit elements; how exact they have to be, the bound alone decides.
A program may use at most 64 MiB of HBM per device.

v0:
```python
import jax
import jax.numpy as jnp
from jax import lax
from jax.sharding import PartitionSpec as P


def padded(block, sides, width):
    for axis, dim in sides:
        count = lax.axis_size(axis)
        forward = [(i, i + 1) for i in range(count - 1)]
        backward = [(target, source) for source, target in forward]
        low = lax.ppermute(
            lax.slice_in_dim(block, block.shape[dim] - width, None, axis=dim), axis, forward
        )
        high = lax.ppermute(lax.slice_in_dim(block, 0, width, axis=dim), axis, backward)
        block = jnp.concatenate([low, block, high], axis=dim)
    return block


def operate(extended, kappa_cols):
    centre = extended[:, 1:-1]
    row_padded = jnp.pad(centre, ((1, 1), (0, 0), (0, 0)))
    beside = row_padded[2:] + row_padded[:-2]
    beside = beside + extended[:, 2:] + extended[:, :-2]
    return (kappa_cols[:, :, None] + 4.0) * centre - beside


def face_halo(field):
    return padded(field, (("space", 1),), 1)


def local(latent, events, log_base, innovation, kappa_sq, chol_factor, step_size):
    row_count, col_count, time_count = latent.shape
    col_index = lax.axis_index("space")
    padded_kappa = jnp.pad(kappa_sq, ((0, 0), (2, 2)))
    first_col = col_index * col_count + 2 - 0
    kappa_here = lax.dynamic_slice(
        padded_kappa, (jnp.int32(0), first_col), (row_count, col_count + 2 * 0)
    )
    first_pass = operate(face_halo(latent), kappa_here)
    spatial = operate(face_halo(first_pass), kappa_here)
    cell_count = row_count * col_count
    flattened = spatial.reshape(cell_count, time_count)
    factor_rows = chol_factor
    projected = jnp.dot(
        lax.all_gather(flattened, "tm", axis=1, tiled=True),
        factor_rows,
        precision=lax.Precision.HIGHEST,
        preferred_element_type=jnp.float32,
    )
    factor_rows = chol_factor
    by_hour = lax.psum_scatter(
        lax.dot_general(
            factor_rows,
            projected,
            (((1,), (1,)), ((), ())),
            precision=lax.Precision.HIGHEST,
            preferred_element_type=jnp.float32,
        ),
        "tm",
        scatter_dimension=0,
        tiled=True,
    )
    prior_term = by_hour.T.reshape(row_count, col_count, time_count)
    gradient = events.astype(jnp.float32) - jnp.exp(log_base + latent) - prior_term
    proposal = latent + step_size[0] * gradient + jnp.sqrt(2.0 * step_size[0]) * innovation
    return (gradient, proposal)


def solution(mesh):
    in_specs = (
        P(None, "space", "tm"),
        P(None, "space", "tm"),
        P(None, "space", "tm"),
        P(None, "space", "tm"),
        P(),
        P(None, "tm"),
        P(),
    )
    out_specs = (P(None, "space", "tm"), P(None, "space", "tm"))
    return jax.shard_map(local, mesh=mesh, in_specs=in_specs, out_specs=out_specs, check_vma=False)
```

profile of v0, /device:TPU:1, one launch (start us, length us, event | category | flops | bytes accessed | tf_op | source)
XLA Modules:
  0.0 295.5 jit_solution(11682274919811678598)
XLA Ops:
  7.2 0.0 copy-start
  7.2 0.0 all-gather.2.cloned.1.call-start
  7.2 1.0 fusion.10
  8.3 1.3 collective-permute-start
  9.6 6.4 %collective-permute-start.1 = (f32[24,1,128]{2,1,0:T(1,128)S(1)}, f32[24,1,128]{2,1,0:T(1,128)S(1)}, u32[]{:S(2)}, u32[]{:S(2)}) collective-permute-start(f32[24,1,128]{2,1,0:T(1,128)S(1)} %get-tuple-element.7), channel_id=1, source_target_pairs={{0,16},{16,32},{32,48},{48,64},{64,80},{80,96},{96,112},{112,128},... | collective-permute-start | bytes 36872 | tf_op jit(solution)/shard_map/ppermute | solution.py:12
  15.9 0.9 fusion.8
  16.8 0.0 collective-permute-done
  16.8 0.0 collective-permute-done.1
  16.8 2.9 fusion.3
  19.7 1.3 collective-permute-start.2
  21.0 6.7 %collective-permute-start.3 = (f32[24,1,128]{2,1,0:T(1,128)S(1)}, f32[24,1,128]{2,1,0:T(1,128)S(1)}, u32[]{:S(2)}, u32[]{:S(2)}) collective-permute-start(f32[24,1,128]{2,1,0:T(1,128)S(1)} %get-tuple-element.5), channel_id=1, source_target_pairs={{0,16},{16,32},{32,48},{48,64},{64,80},{80,96},{96,112},{112,128},... | collective-permute-start | bytes 36872 | tf_op jit(solution)/shard_map/ppermute | solution.py:12
  27.8 0.0 collective-permute-done.2
  27.8 0.8 collective-permute-done.3
  28.6 1.2 fusion.7
  29.8 0.0 all-gather.2.cloned.1.call-update
  29.8 0.0 reduce-scatter.2.cloned.1.call-start
  29.8 90.5 %all-gather.2.cloned.1.call-done = f32[1536,2048]{1,0:T(8,128)} async-done(((f32[1536,128]{1,0:T(8,128)}), f32[1536,2048]{1,0:T(8,128)}) %all-gather.2.cloned.1.call-update) | async-done | bytes 12582928 | tf_op jit(solution)/shard_map/all_gather | solution.py:46
  120.3 0.0 copy-done
  120.3 12.5 %fusion.11 = f32[1536,128]{1,0:T(8,128)S(1)} fusion(f32[1536,2048]{1,0:T(8,128)} %all-gather.2.cloned.1.call-done, f32[2048,128]{1,0:T(8,128)S(1)} %copy-done), kind=kOutput, calls=%fused_computation.23 | convolution fusion | flops 4831838208 | bytes 14417920 | tf_op jit(solution)/shard_map/dot_general | solution.py:45
  132.8 0.0 copy-start.1
  132.8 0.0 copy-start.2
  132.8 0.0 copy-start.3
  132.8 12.3 %convolution_bitcast_fusion = f32[2048,1536]{0,1:T(8,128)} fusion(f32[1536,128]{1,0:T(8,128)S(1)} %fusion.11, f32[2048,128]{1,0:T(8,128)S(1)} %copy-done), kind=kOutput, calls=%fused_computation | convolution fusion | flops 4831838208 | bytes 14417920 | tf_op jit(solution)/shard_map/dot_general | solution.py:53
  145.1 0.0 reduce-scatter.2.cloned.1.call-update
  145.8 139.9 %reduce-scatter.2.cloned.1.call-done = f32[128,1536]{0,1:T(8,128)} async-done(((f32[2048,1536]{0,1:T(8,128)}), f32[128,1536]{0,1:T(8,128)}) %reduce-scatter.2.cloned.1.call-update) | async-done | bytes 786448 | tf_op jit(solution)/shard_map/reduce_scatter | solution.py:52
  285.8 0.0 copy-done.1
  285.8 0.0 copy-done.2
  285.8 0.0 copy-done.3
  285.8 2.9 multiply_add_fusion
  (1 shorter events, 0.0 us)
Async XLA Ops:
  7.2 113.1 %copy-start = (f32[2048,128]{1,0:T(8,128)S(1)}, f32[2048,128]{1,0:T(8,128)}, u32[]{:S(2)}) copy-start(f32[2048,128]{1,0:T(8,128)} %param.12) | copy-start | bytes 3145732
  7.2 113.1 %all-gather.2.cloned.1.call-start = ((), (), s32[]{:S(2)}) async-start(), calls=%async_computation.1 | async-start | bytes 13369344 | tf_op jit(solution)/shard_map/all_gather | solution.py:46
  8.3 8.5 %collective-permute-start = (f32[24,1,128]{2,1,0:T(1,128)S(1)}, f32[24,1,128]{2,1,0:T(1,128)S(1)}, u32[]{:S(2)}, u32[]{:S(2)}) collective-permute-start(f32[24,1,128]{2,1,0:T(1,128)S(1)} %get-tuple-element.6), channel_id=1, source_target_pairs={{16,0},{32,16},{48,32},{64,48},{80,64},{96,80},{112,96},{128,112},... | collective-permute-start | bytes 36872 | tf_op jit(solution)/shard_map/ppermute | solution.py:15
  9.6 7.2 %collective-permute-start.1 = (f32[24,1,128]{2,1,0:T(1,128)S(1)}, f32[24,1,128]{2,1,0:T(1,128)S(1)}, u32[]{:S(2)}, u32[]{:S(2)}) collective-permute-start(f32[24,1,128]{2,1,0:T(1,128)S(1)} %get-tuple-element.7), channel_id=1, source_target_pairs={{0,16},{16,32},{32,48},{48,64},{64,80},{80,96},{96,112},{112,128},... | collective-permute-start | bytes 36872 | tf_op jit(solution)/shard_map/ppermute | solution.py:12
  19.7 8.0 %collective-permute-start.2 = (f32[24,1,128]{2,1,0:T(1,128)S(1)}, f32[24,1,128]{2,1,0:T(1,128)S(1)}, u32[]{:S(2)}, u32[]{:S(2)}) collective-permute-start(f32[24,1,128]{2,1,0:T(1,128)S(1)} %get-tuple-element.4), channel_id=1, source_target_pairs={{16,0},{32,16},{48,32},{64,48},{80,64},{96,80},{112,96},{128,112},... | collective-permute-start | bytes 36872 | tf_op jit(solution)/shard_map/ppermute | solution.py:15
  21.0 7.6 %collective-permute-start.3 = (f32[24,1,128]{2,1,0:T(1,128)S(1)}, f32[24,1,128]{2,1,0:T(1,128)S(1)}, u32[]{:S(2)}, u32[]{:S(2)}) collective-permute-start(f32[24,1,128]{2,1,0:T(1,128)S(1)} %get-tuple-element.5), channel_id=1, source_target_pairs={{0,16},{16,32},{32,48},{48,64},{64,80},{80,96},{96,112},{112,128},... | collective-permute-start | bytes 36872 | tf_op jit(solution)/shard_map/ppermute | solution.py:12
  29.8 256.0 %reduce-scatter.2.cloned.1.call-start = ((), (), s32[]{:S(2)}) async-start(), calls=%async_computation.2 | async-start | bytes 13369344 | tf_op jit(solution)/shard_map/reduce_scatter | solution.py:52
  132.8 153.0 %copy-start.1 = (f32[24,64,128]{2,1,0:T(8,128)S(1)}, f32[24,64,128]{2,1,0:T(8,128)}, u32[]{:S(2)}) copy-start(f32[24,64,128]{2,1,0:T(8,128)} %param.7) | copy-start | bytes 2359300
  132.8 153.0 %copy-start.2 = (f32[24,64,128]{2,1,0:T(8,128)S(1)}, f32[24,64,128]{2,1,0:T(8,128)}, u32[]{:S(2)}) copy-start(f32[24,64,128]{2,1,0:T(8,128)} %param.10) | copy-start | bytes 2359300
  132.8 153.0 %copy-start.3 = (f32[24,64,128]{2,1,0:T(8,128)S(1)}, f32[24,64,128]{2,1,0:T(8,128)}, u32[]{:S(2)}) copy-start(f32[24,64,128]{2,1,0:T(8,128)} %param.9) | copy-start | bytes 2359300
Sparse Core Ops, SparseCore 0:
  29.9 90.3 all-gather.1
  145.2 140.4 reduce-scatter.1
where the time goes:
time: 297 us; the launch traced here: 296 us
  waiting for transfers between devices  231 us (78%)
  matrix products  24.8 us (8%)
  starting transfers between devices  15.8 us (5%)
  between operations  14.8 us (5%)
  other arithmetic  7.85 us (3%)
    reduce_scatter x1, waiting for transfers between devices, local(): lax.psum_scatter(lax.dot_general(factor_rows, projected, (((1,), (1,)), (...  140 us
    all_gather x1, waiting for transfers between devices, local(): lax.all_gather(flattened, 'tm', axis=1, tiled=True)  90.5 us
    ppermute x2, starting transfers between devices, padded(): lax.ppermute(lax.slice_in_dim(block, block.shape[dim] - width, None, axis...  13.1 us
    dot_general x1, matrix products, local(): jnp.dot(lax.all_gather(flattened, 'tm', axis=1, tiled=True), factor_rows,...  12.5 us
    dot_general x1, matrix products, local(): lax.dot_general(factor_rows, projected, (((1,), (1,)), ((), ())), precisi...  12.3 us
  transfers between devices with their start and end apart: 6, of which 3 were waited for; matrix products, arithmetic and copies ran while one was open for 0% of the time, Pallas kernels for 0%

commit v1 on v0

v1 whole, which is shorter than its diff:
```python
import jax
import jax.numpy as jnp
from jax import lax
from jax.sharding import PartitionSpec as P


def halo(block, width):
    count = lax.axis_size("space")
    forward = [(i, i + 1) for i in range(count - 1)]
    backward = [(target, source) for source, target in forward]
    cols = block.shape[1]
    low = lax.ppermute(lax.slice_in_dim(block, cols - width, None, axis=1), "space", forward)
    high = lax.ppermute(lax.slice_in_dim(block, 0, width, axis=1), "space", backward)
    return jnp.concatenate([low, block, high], axis=1)


def operate(extended, kappa_cols):
    centre = extended[:, 1:-1]
    row_padded = jnp.pad(centre, ((1, 1), (0, 0), (0, 0)))
    beside = row_padded[2:] + row_padded[:-2]
    beside = beside + extended[:, 2:] + extended[:, :-2]
    return (kappa_cols[:, :, None] + 4.0) * centre - beside


def gather_factor(chol_cols):
    n = lax.axis_size("tm")
    T, B = chol_cols.shape
    H = (n + 1) * B // 2
    tail = T - H
    j = lax.axis_index("tm")
    pairs = [(i, n - 1 - i) for i in range(n // 2)]
    sent = lax.ppermute(chol_cols[T - tail:], "tm", pairs)
    own_low = lax.dynamic_slice_in_dim(chol_cols, j * B, H, axis=0)
    partner = n - 1 - j
    length = (n - partner) * B - H
    shifted = lax.dynamic_slice_in_dim(
        jnp.concatenate([sent, jnp.zeros((H, B), sent.dtype)], axis=0), tail - length, H, axis=0
    )
    own_tail = chol_cols[T - H:]
    rows = lax.broadcasted_iota(jnp.int32, (H, B), 0)
    own_high = jnp.where(rows < length, shifted, own_tail)
    piece = jnp.where(j < n // 2, own_low, own_high)
    gathered = lax.all_gather(piece, "tm", axis=0, tiled=False)
    blocks = []
    for c in range(n):
        if c < n // 2:
            p = n - 1 - c
            length_c = (n - c) * B - H
            nonzero = jnp.concatenate([gathered[c], gathered[p, :length_c]], axis=0)
        else:
            p = n - 1 - c
            length_p = (n - p) * B - H
            nonzero = gathered[c, length_p:]
        blocks.append(jnp.concatenate([jnp.zeros((c * B, B), nonzero.dtype), nonzero], axis=0))
    return jnp.concatenate(blocks, axis=1)


def local(latent, events, log_base, innovation, kappa_sq, chol_factor, step_size):
    row_count, col_count, time_count = latent.shape
    space_count = lax.axis_size("space")
    col_index = lax.axis_index("space")
    padded_kappa = jnp.pad(kappa_sq, ((0, 0), (1, 1)))
    kappa_wide = lax.dynamic_slice(
        padded_kappa, (jnp.int32(0), col_index * col_count), (row_count, col_count + 2)
    )
    full = gather_factor(chol_factor)
    extended = halo(latent, 2)
    first_pass = operate(extended, kappa_wide)
    cols = lax.broadcasted_iota(jnp.int32, (1, col_count + 2, 1), 1)
    outside = ((cols == 0) & (col_index == 0)) | ((cols == col_count + 1) & (col_index == space_count - 1))
    first_pass = jnp.where(outside, 0.0, first_pass)
    spatial = operate(first_pass, kappa_wide[:, 1:-1])
    cell_count = row_count * col_count
    flattened = spatial.reshape(cell_count, time_count)
    by_cell = lax.all_to_all(flattened, "tm", 0, 1, tiled=True)
    projected = jnp.dot(
        by_cell, full, precision=lax.Precision.HIGHEST, preferred_element_type=jnp.float32
    )
    prior_cells = lax.dot_general(
        projected,
        full,
        (((1,), (1,)), ((), ())),
        precision=lax.Precision.HIGHEST,
        preferred_element_type=jnp.float32,
    )
    prior = lax.all_to_all(prior_cells, "tm", 1, 0, tiled=True)
    prior_term = prior.reshape(row_count, col_count, time_count)
    gradient = events.astype(jnp.float32) - jnp.exp(log_base + latent) - prior_term
    proposal = latent + step_size[0] * gradient + jnp.sqrt(2.0 * step_size[0]) * innovation
    return (gradient, proposal)


def solution(mesh):
    in_specs = (
        P(None, "space", "tm"),
        P(None, "space", "tm"),
        P(None, "space", "tm"),
        P(None, "space", "tm"),
        P(),
        P(None, "tm"),
        P(),
    )
    out_specs = (P(None, "space", "tm"), P(None, "space", "tm"))
    return jax.shard_map(local, mesh=mesh, in_specs=in_specs, out_specs=out_specs, check_vma=False)
```

time: 297 us -> 199 us (0.67)
  waiting for transfers between devices: 231 us -> 71.3 us
  local copies, waits for them, and re-layouts: 1.09 us -> 29.8 us
  other arithmetic: 7.85 us -> 21.5 us
  starting transfers between devices: 15.8 us -> 26.5 us
  matrix products: 24.8 us -> 33.3 us
    reduce_scatter x1 -> x0, waiting for transfers between devices: 140 us -> none  [local(): lax.psum_scatter(lax.dot_general(factor_rows, projected, (((1,), (1,)), (...]
    all_gather x1, waiting for transfers between devices: 90.5 us -> 44.7 us  [gather_factor(): gathered = lax.all_gather(piece, 'tm', axis=0, tiled=False)]
    squeeze x0 -> x16, local copies, waits for them, and re-layouts: none -> 15.4 us  [the longest x8 7.81 us: gather_factor(): nonzero = gathered[c, length_p:]]
    ppermute x4 -> x3, waiting for transfers between devices: 0.81 us -> 14.2 us  [the longest x1 11 us: gather_factor(): sent = lax.ppermute(chol_cols[T - tail:], 'tm', pairs)]
    all_to_all x0 -> x2, starting transfers between devices: none -> 12.9 us  [the longest x1 7.71 us: local(): by_cell = lax.all_to_all(flattened, 'tm', 0, 1, tiled=True)]
    all_to_all x0 -> x2, waiting for transfers between devices: none -> 12.3 us  [the longest x1 12.3 us: local(): prior = lax.all_to_all(prior_cells, 'tm', 1, 0, tiled=True)]
    unnamed x0 -> x8, other arithmetic: none -> 10.7 us
    dot_general x2, matrix products: 24.8 us -> 33.3 us  [the longest x1 19.8 us: local(): lax.dot_general(projected, full, (((1,), (1,)), ((), ())), precision=lax....]
  transfers between devices with their start and end apart: 6 -> 6, of which waited for: 3 -> 4; matrix products, arithmetic and copies ran while one was open for 0% -> 22% of each run, Pallas kernels for 0% -> 0%
where the time goes in v1:
time: 199 us; the launch traced here: 197 us
  waiting for transfers between devices  71.3 us (36%)
  matrix products  33.3 us (17%)
  local copies, waits for them, and re-layouts  29.8 us (15%)
  starting transfers between devices  26.5 us (13%)
  other arithmetic  21.5 us (11%)
  between operations  15 us (8%)
    all_gather x1, waiting for transfers between devices, gather_factor(): gathered = lax.all_gather(piece, 'tm', axis=0, tiled=False)  44.7 us
    dot_general x1, matrix products, local(): lax.dot_general(projected, full, (((1,), (1,)), ((), ())), precision=lax....  19.8 us
    dot_general x1, matrix products, local(): jnp.dot(by_cell, full, precision=lax.Precision.HIGHEST, preferred_element...  13.5 us
    all_to_all x1, waiting for transfers between devices, local(): prior = lax.all_to_all(prior_cells, 'tm', 1, 0, tiled=True)  12.3 us
    ppermute x1, waiting for transfers between devices, gather_factor(): sent = lax.ppermute(chol_cols[T - tail:], 'tm', pairs)  11 us
    unnamed x8, other arithmetic  10.7 us
    squeeze x8, local copies, waits for them, and re-layouts, gather_factor(): nonzero = gathered[c, length_p:]  7.81 us
    all_to_all x1, starting transfers between devices, local(): by_cell = lax.all_to_all(flattened, 'tm', 0, 1, tiled=True)  7.71 us
  transfers between devices with their start and end apart: 6, of which 4 were waited for; matrix products, arithmetic and copies ran while one was open for 22% of the time, Pallas kernels for 0%

profile of v1, /device:TPU:1, one launch (start us, length us, event | category | flops | bytes accessed | tf_op | source)
XLA Modules:
  0.0 197.4 jit_solution(2388541145353253370)
XLA Ops:
  7.2 0.0 all-gather.3.cloned.1.call-start
  7.2 1.1 slice.126
  8.3 7.4 %collective-permute-start.2 = (f32[960,128]{1,0:T(8,128)S(1)}, f32[960,128]{1,0:T(8,128)S(1)}, u32[]{:S(2)}, u32[]{:S(2)}) collective-permute-start(f32[960,128]{1,0:T(8,128)S(1)} %slice.126), channel_id=1, source_target_pairs={{0,15},{1,14},{2,13},{3,12},{4,11},{5,10},{6,9},{7,8},{16,31},{17,... | collective-permute-start | bytes 1474568 | tf_op jit(solution)/shard_map/ppermute | solution.py:32
  15.7 11.0 %collective-permute-done.2 = f32[960,128]{1,0:T(8,128)S(1)} collective-permute-done((f32[960,128]{1,0:T(8,128)S(1)}, f32[960,128]{1,0:T(8,128)S(1)}, u32[]{:S(2)}, u32[]{:S(2)}) %collective-permute-start.2) | collective-permute-done | bytes 491552 | tf_op jit(solution)/shard_map/ppermute | solution.py:32
  26.7 2.3 %fusion.13 = f32[1088,128]{1,0:T(8,128)} fusion(s32[]{:T(128)S(6)} %select_n.29, f32[960,128]{1,0:T(8,128)S(1)} %collective-permute-done.2, f32[2048,128]{1,0:T(8,128)} %param.12, s32[]{:T(128)S(6)} %select_n.28, pred[1088]{0:T(1024)(128)(4,1)S(1)} %iota_compare_fusion, pred[]{:T(512)S(6)} %lt.20), kind=kLoop, calls=%fused_computation.40 | loop fusion | flops 278528 | bytes 2163785 | tf_op jit(solution)/shard_map/jit(_where)/select_n | solution.py:42
  28.9 0.0 all-gather.3.cloned.1.call-update
  29.0 1.0 fusion.17
  29.9 4.9 %collective-permute-start = (f32[24,2,128]{2,1,0:T(2,128)S(1)}, f32[24,2,128]{2,1,0:T(2,128)S(1)}, u32[]{:S(2)}, u32[]{:S(2)}) collective-permute-start(f32[24,2,128]{2,1,0:T(2,128)S(1)} %get-tuple-element.12), channel_id=1, source_target_pairs={{0,16},{16,32},{32,48},{48,64},{64,80},{80,96},{96,112},{112,128},... | collective-permute-start | bytes 73736 | tf_op jit(solution)/shard_map/ppermute | solution.py:12
  34.8 1.3 collective-permute-start.1
  36.1 0.8 fusion.14
  37.0 0.8 fusion.15
  38.0 0.0 collective-permute-done
  38.0 3.3 %collective-permute-done.1 = f32[24,2,128]{2,1,0:T(2,128)S(1)} collective-permute-done((f32[24,2,128]{2,1,0:T(2,128)S(1)}, f32[24,2,128]{2,1,0:T(2,128)S(1)}, u32[]{:S(2)}, u32[]{:S(2)}) %collective-permute-start.1) | collective-permute-done | bytes 24608 | tf_op jit(solution)/shard_map/ppermute | solution.py:13
  41.3 1.2 pad_maximum_fusion
  42.5 1.7 fusion.4
  44.2 0.1 slice.160
  44.3 1.2 fusion.8
  45.5 7.7 %all-to-all-start = ((f32[16,96,128]{2,1,0:T(8,128)}), f32[16,96,128]{2,1,0:T(8,128)S(1)}, u32[]{:S(2)}, u32[]{:S(2)}) async-start(f32[16,96,128]{2,1,0:T(8,128)} %bitcast), calls=%async_computation | async-start | bytes 1572864 | tf_op jit(solution)/shard_map/all_to_all | solution.py:75
  53.2 44.7 %all-gather.3.cloned.1.call-done = f32[17408,128]{1,0:T(8,128)} async-done(((f32[1088,128]{1,0:T(8,128)}), f32[17408,128]{1,0:T(8,128)}) %all-gather.3.cloned.1.call-update) | async-done | bytes 8912912 | tf_op jit(solution)/shard_map/all_gather | solution.py:43
  97.9 0.8 slice_bitcast_fusion.15
  98.7 0.9 slice_bitcast_fusion.13
  99.6 0.9 slice_bitcast_fusion.12
  100.5 0.9 slice_bitcast_fusion.11
  101.4 0.9 slice_bitcast_fusion.10
  102.4 1.0 slice_bitcast_fusion.9
  103.4 1.0 slice_bitcast_fusion.8
  104.3 1.0 slice_bitcast_fusion.7
  105.3 1.0 slice_bitcast_fusion.6
  106.3 1.0 slice_bitcast_fusion.5
  107.3 1.0 slice_bitcast_fusion.4
  108.3 1.0 slice_bitcast_fusion.3
  109.4 1.1 slice_bitcast_fusion.2
  110.4 1.1 slice_bitcast_fusion.1
  111.5 1.1 slice_bitcast_fusion
  112.6 2.6 %fusion.16 = (f32[1088,128]{1,0:T(8,128)S(1)}, f32[1088,128]{1,0:T(8,128)S(1)}, f32[1088,128]{1,0:T(8,128)S(1)}, f32[1088,128]{1,0:T(8,128)S(1)}, f32[1088,128]{...) fusion(f32[17408,128]{1,0:T(8,128)} %all-gather.3.cloned.1.call-done), kind=kLoop, calls=%fused_computation.63 | loop fusion | bytes 8912896 | tf_op jit(solution)/shard_map/slice | solution.py:49
  115.1 1.1 maximum_dynamic-update-slice_fusion.7
  116.2 1.4 maximum_dynamic-update-slice_fusion.6
  117.6 1.4 maximum_dynamic-update-slice_fusion.5
  119.0 1.4 maximum_dynamic-update-slice_fusion.4
  120.4 1.4 maximum_dynamic-update-slice_fusion.3
  121.8 1.3 maximum_dynamic-update-slice_fusion.2
  123.1 1.3 maximum_dynamic-update-slice_fusion.1
  124.4 1.4 maximum_dynamic-update-slice_fusion
  125.8 1.1 pad_dynamic-update-slice_fusion.7
  126.9 1.1 pad_dynamic-update-slice_fusion.6
  128.0 1.1 pad_dynamic-update-slice_fusion.5
  129.1 0.8 slice_bitcast_fusion.14
  130.0 1.1 pad_dynamic-update-slice_fusion.4
  131.0 1.1 pad_dynamic-update-slice_fusion.3
  132.1 1.1 pad_dynamic-update-slice_fusion.2
  133.2 1.1 pad_dynamic-update-slice_fusion.1
  134.3 1.1 pad_dynamic-update-slice_fusion
  135.4 0.0 copy-start
  135.4 0.0 copy-start.1
  135.4 0.0 all-to-all-done
  135.4 13.5 %fusion.9 = f32[96,2048]{1,0:T(8,128)S(1)} fusion(f32[2048,2048]{1,0:T(8,128)} %pad_dynamic-update-slice_fusion, f32[16,96,128]{2,1,0:T(8,128)S(1)} %all-to-all-done), kind=kOutput, calls=%fused_computation.33 | convolution fusion | flops 4831838208 | bytes 18350080 | tf_op jit(solution)/shard_map/dot_general | solution.py:76
  148.9 19.8 %convolution_bitcast_fusion = f32[12,16,8,128]{3,2,1,0:T(8,128)S(1)} fusion(f32[96,2048]{1,0:T(8,128)S(1)} %fusion.9, f32[2048,2048]{1,0:T(8,128)} %pad_dynamic-update-slice_fusion), kind=kOutput, calls=%fused_computation | convolution fusion | flops 4831838208 | bytes 18350080 | tf_op jit(solution)/shard_map/dot_general | solution.py:79
  168.7 1.0 copy.21
  169.7 5.2 %all-to-all-start.1 = ((f32[96,16,128]{2,0,1:T(8,128)}), f32[96,16,128]{2,0,1:T(8,128)S(1)}, u32[]{:S(2)}, u32[]{:S(2)}) async-start(f32[96,16,128]{2,0,1:T(8,128)} %bitcast.53), calls=%async_computation.1 | async-start | bytes 1572864 | tf_op jit(solution)/shard_map/all_to_all | solution.py:86
  175.6 12.3 %all-to-all-done.1 = f32[96,16,128]{2,0,1:T(8,128)S(1)} async-done(((f32[96,16,128]{2,0,1:T(8,128)}), f32[96,16,128]{2,0,1:T(8,128)S(1)}, u32[]{:S(2)}, u32[]{:S(2)}) %all-to-all-start.1) | async-done | bytes 786464 | tf_op jit(solution)/shard_map/all_to_all | solution.py:86
  187.9 0.0 copy-done
  187.9 0.0 copy-done.1
  187.9 0.0 copy-done.2
  187.9 2.7 %multiply_add_fusion = (f32[24,64,128]{2,1,0:T(8,128)}, f32[24,64,128]{2,1,0:T(8,128)}) fusion(f32[24,64,128]{2,1,0:T(8,128)S(1)} %copy-done.1, f32[24,64,128]{2,1,0:T(8,128)S(1)} %copy-done, f32[]{:T(128)S(6)} %sqrt.3, f32[]{:T(128)} %bitcast.54, f32[24,64,128]{2,1,0:T(8,128)S(1)} %bitcast.72, f32[24,64,128]{2,1,0:T(8,128)S(1)} %copy-done.2, ...), kind=kLoop, calls=%fused_computation.37 | loop fusion | flops 1572864 | bytes 5505032 | tf_op jit(solution)/shard_map/add | solution.py:89
  (17 shorter events, 0.1 us)
Async XLA Ops:
  7.2 90.8 %all-gather.3.cloned.1.call-start = ((), (), s32[]{:S(2)}) async-start(), calls=%async_computation.2 | async-start | bytes 9469952 | tf_op jit(solution)/shard_map/all_gather | solution.py:43
  8.3 18.4 %collective-permute-start.2 = (f32[960,128]{1,0:T(8,128)S(1)}, f32[960,128]{1,0:T(8,128)S(1)}, u32[]{:S(2)}, u32[]{:S(2)}) collective-permute-start(f32[960,128]{1,0:T(8,128)S(1)} %slice.126), channel_id=1, source_target_pairs={{0,15},{1,14},{2,13},{3,12},{4,11},{5,10},{6,9},{7,8},{16,31},{17,... | collective-permute-start | bytes 1474568 | tf_op jit(solution)/shard_map/ppermute | solution.py:32
  29.9 8.1 %collective-permute-start = (f32[24,2,128]{2,1,0:T(2,128)S(1)}, f32[24,2,128]{2,1,0:T(2,128)S(1)}, u32[]{:S(2)}, u32[]{:S(2)}) collective-permute-start(f32[24,2,128]{2,1,0:T(2,128)S(1)} %get-tuple-element.12), channel_id=1, source_target_pairs={{0,16},{16,32},{32,48},{48,64},{64,80},{80,96},{96,112},{112,128},... | collective-permute-start | bytes 73736 | tf_op jit(solution)/shard_map/ppermute | solution.py:12
  34.8 6.4 %collective-permute-start.1 = (f32[24,2,128]{2,1,0:T(2,128)S(1)}, f32[24,2,128]{2,1,0:T(2,128)S(1)}, u32[]{:S(2)}, u32[]{:S(2)}) collective-permute-start(f32[24,2,128]{2,1,0:T(2,128)S(1)} %get-tuple-element.13), channel_id=1, source_target_pairs={{16,0},{32,16},{48,32},{64,48},{80,64},{96,80},{112,96},{128,112},... | collective-permute-start | bytes 73736 | tf_op jit(solution)/shard_map/ppermute | solution.py:13
  45.5 89.9 %all-to-all-start = ((f32[16,96,128]{2,1,0:T(8,128)}), f32[16,96,128]{2,1,0:T(8,128)S(1)}, u32[]{:S(2)}, u32[]{:S(2)}) async-start(f32[16,96,128]{2,1,0:T(8,128)} %bitcast), calls=%async_computation | async-start | bytes 1572864 | tf_op jit(solution)/shard_map/all_to_all | solution.py:75
  135.4 52.5 %copy-start = (f32[24,64,128]{2,1,0:T(8,128)S(1)}, f32[24,64,128]{2,1,0:T(8,128)}, u32[]{:S(2)}) copy-start(f32[24,64,128]{2,1,0:T(8,128)} %param.7) | copy-start | bytes 2359300
  135.4 52.5 %copy-start.1 = (f32[24,64,128]{2,1,0:T(8,128)S(1)}, f32[24,64,128]{2,1,0:T(8,128)}, u32[]{:S(2)}) copy-start(f32[24,64,128]{2,1,0:T(8,128)} %param.10) | copy-start | bytes 2359300
  135.4 52.5 %copy-start.2 = (f32[24,64,128]{2,1,0:T(8,128)S(1)}, f32[24,64,128]{2,1,0:T(8,128)}, u32[]{:S(2)}) copy-start(f32[24,64,128]{2,1,0:T(8,128)} %param.9) | copy-start | bytes 2359300
  169.7 18.2 %all-to-all-start.1 = ((f32[96,16,128]{2,0,1:T(8,128)}), f32[96,16,128]{2,0,1:T(8,128)S(1)}, u32[]{:S(2)}, u32[]{:S(2)}) async-start(f32[96,16,128]{2,0,1:T(8,128)} %bitcast.53), calls=%async_computation.1 | async-start | bytes 1572864 | tf_op jit(solution)/shard_map/all_to_all | solution.py:86
Sparse Core Ops, SparseCore 0:
  29.1 68.8 all-gather.2

commit v2 on v1

v2 whole, which is shorter than its diff:
```python
import jax
import jax.numpy as jnp
from jax import lax
from jax.sharding import Mesh
from jax.sharding import PartitionSpec as P

TM = ("chip", "core")


def halo(block, width):
    count = lax.axis_size("space")
    forward = [(i, i + 1) for i in range(count - 1)]
    backward = [(target, source) for source, target in forward]
    cols = block.shape[1]
    low = lax.ppermute(lax.slice_in_dim(block, cols - width, None, axis=1), "space", forward)
    high = lax.ppermute(lax.slice_in_dim(block, 0, width, axis=1), "space", backward)
    return jnp.concatenate([low, block, high], axis=1)


def operate(extended, kappa_cols):
    centre = extended[:, 1:-1]
    row_padded = jnp.pad(centre, ((1, 1), (0, 0), (0, 0)))
    beside = row_padded[2:] + row_padded[:-2]
    beside = beside + extended[:, 2:] + extended[:, :-2]
    return (kappa_cols[:, :, None] + 4.0) * centre - beside


def gather_factor(chol_cols):
    g = lax.axis_size("chip")
    cores = lax.axis_size("core")
    T, B = chol_cols.shape
    S = cores * B
    H = (2 * T - (g - 1) * S) // 2
    tail = T - H
    k = lax.axis_index("chip")
    pairs = [(i, g - 1 - i) for i in range(g // 2)]
    sent = lax.ppermute(chol_cols[H:], "chip", pairs)
    own_low = lax.dynamic_slice_in_dim(chol_cols, k * S, H, axis=0)
    partner = g - 1 - k
    length = T - partner * S - H
    shifted = lax.dynamic_slice_in_dim(
        jnp.concatenate([sent, jnp.zeros((H, B), sent.dtype)], axis=0), tail - length, H, axis=0
    )
    own_tail = chol_cols[T - H:]
    rows = lax.broadcasted_iota(jnp.int32, (H, B), 0)
    own_high = jnp.where(rows < length, shifted, own_tail)
    piece = jnp.where(k < g // 2, own_low, own_high)
    gathered = lax.all_gather(piece, "chip", axis=0, tiled=False)
    blocks = []
    for c in range(g):
        p = g - 1 - c
        if c < g // 2:
            length_c = T - c * S - H
            nonzero = jnp.concatenate([gathered[c], gathered[p, :length_c]], axis=0)
        else:
            length_p = T - p * S - H
            nonzero = gathered[c, length_p:]
        blocks.append(jnp.concatenate([jnp.zeros((c * S, B), nonzero.dtype), nonzero], axis=0))
    return jnp.stack(blocks, axis=0)


def local(latent, events, log_base, innovation, kappa_sq, chol_factor, step_size):
    row_count, col_count, time_count = latent.shape
    g = lax.axis_size("chip")
    cores = lax.axis_size("core")
    space_count = lax.axis_size("space")
    col_index = lax.axis_index("space")
    padded_kappa = jnp.pad(kappa_sq, ((0, 0), (1, 1)))
    kappa_wide = lax.dynamic_slice(
        padded_kappa, (jnp.int32(0), col_index * col_count), (row_count, col_count + 2)
    )
    factor = gather_factor(chol_factor)
    extended = halo(latent, 2)
    first_pass = operate(extended, kappa_wide)
    cols = lax.broadcasted_iota(jnp.int32, (1, col_count + 2, 1), 1)
    outside = ((cols == 0) & (col_index == 0)) | ((cols == col_count + 1) & (col_index == space_count - 1))
    first_pass = jnp.where(outside, 0.0, first_pass)
    spatial = operate(first_pass, kappa_wide[:, 1:-1])
    cell_count = row_count * col_count
    group = cell_count // g
    flattened = spatial.reshape(cell_count, time_count)
    by_chip = lax.all_to_all(flattened, "chip", 0, 1, tiled=True)
    both = lax.all_gather(by_chip.reshape(group, g, time_count), "core", axis=0, tiled=False)
    hours = jnp.transpose(both, (1, 2, 0, 3)).reshape(group, g * cores * time_count)
    projected = lax.dot_general(
        hours, factor, (((1,), (1,)), ((), ())),
        precision=lax.Precision.HIGHEST, preferred_element_type=jnp.float32,
    )
    partial = lax.dot_general(
        projected, factor, (((1, 2), (0, 2)), ((), ())),
        precision=lax.Precision.HIGHEST, preferred_element_type=jnp.float32,
    )
    split = jnp.transpose(partial.reshape(group, g, cores, time_count), (2, 0, 1, 3))
    summed = lax.psum_scatter(split, "core", scatter_dimension=0, tiled=True)[0]
    prior = lax.all_to_all(summed, "chip", 1, 0, tiled=True)
    prior_term = prior.reshape(row_count, col_count, time_count)
    gradient = events.astype(jnp.float32) - jnp.exp(log_base + latent) - prior_term
    proposal = latent + step_size[0] * gradient + jnp.sqrt(2.0 * step_size[0]) * innovation
    return (gradient, proposal)


def solution(mesh):
    space = mesh.shape["space"]
    tm = mesh.shape["tm"]
    view = Mesh(mesh.devices.reshape(space, tm // 2, 2), ("space", "chip", "core"))
    big = P(None, "space", TM)
    in_specs = (big, big, big, big, P(), P(None, TM), P())
    out_specs = (big, big)
    return jax.shard_map(local, mesh=view, in_specs=in_specs, out_specs=out_specs, check_vma=False)
```

time: 199 us -> 238 us (1.20)
  waiting for transfers between devices: 71.3 us -> 145 us
  matrix products: 33.3 us -> 15.5 us
  blocking collectives: 0 us -> 15.1 us
  other arithmetic: 21.5 us -> 10 us
  starting transfers between devices: 26.5 us -> 15.6 us
  local copies, waits for them, and re-layouts: 29.8 us -> 21 us
    all_gather x1 -> x2, waiting for transfers between devices: 44.7 us -> 106 us  [the longest x1 102 us: gather_factor(): gathered = lax.all_gather(piece, 'chip', axis=0, tiled=False)]
    dot_general x2, matrix products: 33.3 us -> 15.5 us  [the longest x1 9.93 us: local(): lax.dot_general(projected, factor, (((1, 2), (0, 2)), ((), ())), precisio...]
    reduce_scatter x0 -> x1, waiting for transfers between devices: none -> 15.6 us  [local(): summed = lax.psum_scatter(split, 'core', scatter_dimension=0, tiled=True)[0]]
    all_to_all x0 -> x1, blocking collectives: none -> 15.1 us  [local(): by_chip = lax.all_to_all(flattened, 'chip', 0, 1, tiled=True)]
    unnamed x8 -> x4, other arithmetic: 10.7 us -> 1.07 us
    all_to_all x2 -> x1, starting transfers between devices: 12.9 us -> 4.76 us  [local(): prior = lax.all_to_all(summed, 'chip', 1, 0, tiled=True)]
    unnamed x13 -> x9, local copies, waits for them, and re-layouts: 7.64 us -> 0.23 us
    reshape x0 -> x3, local copies, waits for them, and re-layouts: none -> 5.16 us  [the longest x2 3.9 us: local(): partial.reshape(group, g, cores, time_count)]
  transfers between devices with their start and end apart: 6 -> 7, of which waited for: 4 -> 6; matrix products, arithmetic and copies ran while one was open for 22% -> 3% of each run, Pallas kernels for 0% -> 0%
where the time goes in v2:
time: 238 us; the launch traced here: 237 us
  waiting for transfers between devices  145 us (61%)
  local copies, waits for them, and re-layouts  21 us (9%)
  starting transfers between devices  15.6 us (7%)
  matrix products  15.5 us (7%)
  blocking collectives  15.1 us (6%)
  between operations  14.7 us (6%)
  other arithmetic  10 us (4%)
    all_gather x1, waiting for transfers between devices, gather_factor(): gathered = lax.all_gather(piece, 'chip', axis=0, tiled=False)  102 us
    reduce_scatter x1, waiting for transfers between devices, local(): summed = lax.psum_scatter(split, 'core', scatter_dimension=0, tiled=True)[0]  15.6 us
    all_to_all x1, blocking collectives, local(): by_chip = lax.all_to_all(flattened, 'chip', 0, 1, tiled=True)  15.1 us
    all_to_all x1, waiting for transfers between devices, local(): prior = lax.all_to_all(summed, 'chip', 1, 0, tiled=True)  11.8 us
    dot_general x1, matrix products, local(): lax.dot_general(projected, factor, (((1, 2), (0, 2)), ((), ())), precisio...  9.93 us
    ppermute x1, waiting for transfers between devices, gather_factor(): sent = lax.ppermute(chol_cols[H:], 'chip', pairs)  7.07 us
    ppermute x1, starting transfers between devices, halo(): lax.ppermute(lax.slice_in_dim(block, cols - width, None, axis=1), 'space'...  5.73 us
    dot_general x1, matrix products, local(): lax.dot_general(hours, factor, (((1,), (1,)), ((), ())), precision=lax.Pr...  5.58 us
  transfers between devices with their start and end apart: 7, of which 6 were waited for; matrix products, arithmetic and copies ran while one was open for 3% of the time, Pallas kernels for 0%

profile of v2, /device:TPU:1, one launch (start us, length us, event | category | flops | bytes accessed | tf_op | source)
XLA Modules:
  0.0 237.1 jit_solution(16552910394981069210)
XLA Ops:
  7.2 0.0 copy-start.1
  7.2 0.0 all-gather.5.cloned.1.call-start
  7.2 1.0 fusion.18
  8.3 5.7 %collective-permute-start = (f32[24,2,128]{2,1,0:T(2,128)S(1)}, f32[24,2,128]{2,1,0:T(2,128)S(1)}, u32[]{:S(2)}, u32[]{:S(2)}) collective-permute-start(f32[24,2,128]{2,1,0:T(2,128)S(1)} %get-tuple-element.8), channel_id=1, source_target_pairs={{0,16},{16,32},{32,48},{48,64},{64,80},{80,96},{96,112},{112,128},... | collective-permute-start | bytes 73736 | tf_op jit(solution)/shard_map/ppermute | solution.py:15
  14.0 1.3 collective-permute-start.1
  15.3 0.8 fusion.15
  16.1 0.8 fusion.16
  17.0 0.0 collective-permute-done
  17.0 4.3 %collective-permute-done.1 = f32[24,2,128]{2,1,0:T(2,128)S(1)} collective-permute-done((f32[24,2,128]{2,1,0:T(2,128)S(1)}, f32[24,2,128]{2,1,0:T(2,128)S(1)}, u32[]{:S(2)}, u32[]{:S(2)}) %collective-permute-start.1) | collective-permute-done | bytes 24608 | tf_op jit(solution)/shard_map/ppermute | solution.py:16
  21.3 1.2 pad_maximum_fusion
  22.5 1.7 fusion.8
  24.3 0.1 slice.108
  24.4 0.3 fusion.12
  24.7 15.1 %all_to_all.31 = f32[8,192,128]{2,1,0:T(8,128)} all-to-all(f32[8,192,128]{2,1,0:T(8,128)S(1)} %bitcast.74), channel_id=1, replica_groups=mesh['space'=16,'chip'=8,'core'=2] {'chip'}, dimensions={0} | all-to-all | bytes 1572864 | tf_op jit(solution)/shard_map/all_to_all | solution.py:82
  39.8 0.0 all-gather.5.cloned.1.call-update
  39.8 0.0 all-gather.7.cloned.1.call-start
  39.9 0.0 copy-done.1
  39.9 3.7 %collective-permute-start.2 = (f32[896,128]{1,0:T(8,128)S(1)}, f32[896,128]{1,0:T(8,128)S(1)}, u32[]{:S(2)}, u32[]{:S(2)}) collective-permute-start(f32[896,128]{1,0:T(8,128)S(1)} %slice.90), channel_id=1, source_target_pairs={{0,14},{2,12},{4,10},{6,8},{1,15},{3,13},{5,11},{7,9},{16,30},{18,... | collective-permute-start | bytes 1376264 | tf_op jit(solution)/shard_map/ppermute | solution.py:37
  43.7 7.1 %collective-permute-done.2 = f32[896,128]{1,0:T(8,128)S(1)} collective-permute-done((f32[896,128]{1,0:T(8,128)S(1)}, f32[896,128]{1,0:T(8,128)S(1)}, u32[]{:S(2)}, u32[]{:S(2)}) %collective-permute-start.2) | collective-permute-done | bytes 458784 | tf_op jit(solution)/shard_map/ppermute | solution.py:37
  50.7 1.1 fusion.14
  51.8 0.0 all-gather.7.cloned.1.call-update
  51.8 0.0 reduce-scatter.2.cloned.1.call-start
  52.0 4.4 %all-gather.5.cloned.1.call-done = f32[384,8,128]{2,0,1:T(8,128)} async-done(((f32[192,8,128]{2,0,1:T(8,128)}), f32[384,8,128]{2,0,1:T(8,128)}) %all-gather.5.cloned.1.call-update) | async-done | bytes 1572880 | tf_op jit(solution)/shard_map/all_gather | solution.py:83
  56.4 2.6 %copy.17 = f32[192,8,2,128]{3,2,1,0:T(2,128)S(1)} copy(f32[192,8,2,128]{3,0,2,1:T(8,128)} %bitcast.76) | data formatting | bytes 3145728 | tf_op jit(solution)/shard_map/transpose | solution.py:84
  59.0 1.3 reshape.52
  60.3 101.8 %all-gather.7.cloned.1.call-done = f32[9216,128]{1,0:T(8,128)} async-done(((f32[1152,128]{1,0:T(8,128)}), f32[9216,128]{1,0:T(8,128)}) %all-gather.7.cloned.1.call-update) | async-done | bytes 4718608 | tf_op jit(solution)/shard_map/all_gather | solution.py:48
  162.1 0.8 slice_bitcast_fusion.7
  163.0 0.9 slice_bitcast_fusion.6
  163.9 0.9 slice_bitcast_fusion.5
  164.8 1.0 slice_bitcast_fusion.4
  165.8 1.0 slice_bitcast_fusion.3
  166.8 1.0 slice_bitcast_fusion.2
  167.8 1.1 slice_bitcast_fusion.1
  168.9 1.1 slice_bitcast_fusion
  170.0 1.8 fusion.17
  171.7 0.1 fusion
  171.8 0.3 fusion.1
  172.1 0.3 fusion.2
  172.5 0.3 fusion.3
  172.8 0.1 bitcast_dynamic-update-slice_fusion.3
  172.9 0.1 bitcast_dynamic-update-slice_fusion.2
  173.0 0.1 bitcast_dynamic-update-slice_fusion.1
  173.1 0.1 bitcast_dynamic-update-slice_fusion
  173.1 5.6 %fusion.19 = f32[192,8,128]{2,0,1:T(8,128)S(1)} fusion(f32[192,2048,1]{1,0,2:T(8,128)S(1)} %reshape.52, f32[8,2048,128]{2,1,0:T(8,128)S(1)} %bitcast_dynamic-update-slice_fusion), kind=kOutput, calls=%fused_computation.50 | convolution fusion | flops 4831838208 | bytes 10747904 | tf_op jit(solution)/shard_map/dot_general | solution.py:85
  178.7 0.0 copy-start
  178.7 0.0 copy-start.2
  178.7 9.9 %convolution_bitcast_fusion = f32[192,2048]{1,0:T(8,128)} fusion(f32[192,8,128]{2,0,1:T(8,128)S(1)} %fusion.19, f32[8,2048,128]{2,1,0:T(8,128)S(1)} %bitcast_dynamic-update-slice_fusion), kind=kOutput, calls=%fused_computation | convolution fusion | flops 4831838208 | bytes 10747904 | tf_op jit(solution)/shard_map/dot_general | solution.py:89
  188.7 2.6 %reshape.40 = f32[192,8,2,128]{3,2,1,0:T(2,128)S(1)} reshape(f32[192,2048]{1,0:T(8,128)} %convolution_bitcast_fusion) | data formatting | bytes 3145728 | tf_op jit(solution)/shard_map/reshape | solution.py:93
  191.3 1.3 copy.22
  192.6 0.0 reduce-scatter.2.cloned.1.call-update
  192.6 15.6 %reduce-scatter.2.cloned.1.call-done = f32[1,192,8,128]{3,2,1,0:T(8,128)} async-done(((f32[2,192,8,128]{3,2,1,0:T(8,128)}), f32[1,192,8,128]{3,2,1,0:T(8,128)}) %reduce-scatter.2.cloned.1.call-update) | async-done | bytes 786448 | tf_op jit(solution)/shard_map/reduce_scatter | solution.py:94
  208.2 2.2 copy.19
  210.3 4.8 %all-to-all-start.1 = ((f32[192,8,128]{2,0,1:T(8,128)}), f32[192,8,128]{2,0,1:T(8,128)S(1)}, u32[]{:S(2)}, u32[]{:S(2)}) async-start(f32[192,8,128]{2,0,1:T(8,128)} %copy.19), calls=%async_computation.2 | async-start | bytes 1572864 | tf_op jit(solution)/shard_map/all_to_all | solution.py:95
  215.8 11.8 %all-to-all-done.1 = f32[192,8,128]{2,0,1:T(8,128)S(1)} async-done(((f32[192,8,128]{2,0,1:T(8,128)}), f32[192,8,128]{2,0,1:T(8,128)S(1)}, u32[]{:S(2)}, u32[]{:S(2)}) %all-to-all-start.1) | async-done | bytes 786464 | tf_op jit(solution)/shard_map/all_to_all | solution.py:95
  227.6 0.0 copy-done
  227.6 0.0 copy-done.2
  227.6 2.9 %multiply_add_fusion = (f32[24,64,128]{2,1,0:T(8,128)}, f32[24,64,128]{2,1,0:T(8,128)}) fusion(f32[24,64,128]{2,1,0:T(8,128)S(1)} %copy-done.2, f32[24,64,128]{2,1,0:T(8,128)S(1)} %copy-done, f32[]{:T(128)S(6)} %sqrt.3, f32[]{:T(128)} %bitcast.62, f32[24,64,128]{2,1,0:T(8,128)S(1)} %bitcast.75, f32[24,64,128]{2,1,0:T(8,128)} %param.9, s32[24,64,128]{2,1,0:T(8,128)} %param.8), kind=kLoop, calls=%fused_computation.30 | loop fusion | flops 1572864 | bytes 5505032 | tf_op jit(solution)/shard_map/add | solution.py:98
  (9 shorter events, 0.1 us)
Async XLA Ops:
  7.2 32.7 %copy-start.1 = (f32[2048,128]{1,0:T(8,128)S(1)}, f32[2048,128]{1,0:T(8,128)}, u32[]{:S(2)}) copy-start(f32[2048,128]{1,0:T(8,128)} %param.12) | copy-start | bytes 3145732
  7.2 49.2 %all-gather.5.cloned.1.call-start = ((), (), s32[]{:S(2)}) async-start(), calls=%async_computation.4 | async-start | bytes 2359296 | tf_op jit(solution)/shard_map/all_gather | solution.py:83
  8.3 8.7 %collective-permute-start = (f32[24,2,128]{2,1,0:T(2,128)S(1)}, f32[24,2,128]{2,1,0:T(2,128)S(1)}, u32[]{:S(2)}, u32[]{:S(2)}) collective-permute-start(f32[24,2,128]{2,1,0:T(2,128)S(1)} %get-tuple-element.8), channel_id=1, source_target_pairs={{0,16},{16,32},{32,48},{48,64},{64,80},{80,96},{96,112},{112,128},... | collective-permute-start | bytes 73736 | tf_op jit(solution)/shard_map/ppermute | solution.py:15
  14.0 7.3 %collective-permute-start.1 = (f32[24,2,128]{2,1,0:T(2,128)S(1)}, f32[24,2,128]{2,1,0:T(2,128)S(1)}, u32[]{:S(2)}, u32[]{:S(2)}) collective-permute-start(f32[24,2,128]{2,1,0:T(2,128)S(1)} %get-tuple-element.9), channel_id=1, source_target_pairs={{16,0},{32,16},{48,32},{64,48},{80,64},{96,80},{112,96},{128,112},... | collective-permute-start | bytes 73736 | tf_op jit(solution)/shard_map/ppermute | solution.py:16
  39.8 122.3 %all-gather.7.cloned.1.call-start = ((), (), s32[]{:S(2)}) async-start(), calls=%async_computation.5 | async-start | bytes 5308416 | tf_op jit(solution)/shard_map/all_gather | solution.py:48
  39.9 10.8 %collective-permute-start.2 = (f32[896,128]{1,0:T(8,128)S(1)}, f32[896,128]{1,0:T(8,128)S(1)}, u32[]{:S(2)}, u32[]{:S(2)}) collective-permute-start(f32[896,128]{1,0:T(8,128)S(1)} %slice.90), channel_id=1, source_target_pairs={{0,14},{2,12},{4,10},{6,8},{1,15},{3,13},{5,11},{7,9},{16,30},{18,... | collective-permute-start | bytes 1376264 | tf_op jit(solution)/shard_map/ppermute | solution.py:37
  51.8 156.3 %reduce-scatter.2.cloned.1.call-start = ((), (), s32[]{:S(2)}) async-start(), calls=%async_computation.3 | async-start | bytes 2359296 | tf_op jit(solution)/shard_map/reduce_scatter | solution.py:94
  178.7 48.9 %copy-start = (f32[24,64,128]{2,1,0:T(8,128)S(1)}, f32[24,64,128]{2,1,0:T(8,128)}, u32[]{:S(2)}) copy-start(f32[24,64,128]{2,1,0:T(8,128)} %param.7) | copy-start | bytes 2359300
  178.7 48.9 %copy-start.2 = (f32[24,64,128]{2,1,0:T(8,128)S(1)}, f32[24,64,128]{2,1,0:T(8,128)}, u32[]{:S(2)}) copy-start(f32[24,64,128]{2,1,0:T(8,128)} %param.10) | copy-start | bytes 2359300
  210.3 17.3 %all-to-all-start.1 = ((f32[192,8,128]{2,0,1:T(8,128)}), f32[192,8,128]{2,0,1:T(8,128)S(1)}, u32[]{:S(2)}, u32[]{:S(2)}) async-start(f32[192,8,128]{2,0,1:T(8,128)} %copy.19), calls=%async_computation.2 | async-start | bytes 1572864 | tf_op jit(solution)/shard_map/all_to_all | solution.py:95
Sparse Core Ops, SparseCore 0:
  40.0 16.3 all-gather.4
  58.8 103.3 all-gather.6
  192.7 15.4 reduce-scatter.1

commit v3 on v2

--- a/solution.py
+++ b/solution.py
@@ -1,10 +1,13 @@
 import jax
 import jax.numpy as jnp
 from jax import lax
+from jax.experimental import pallas as pl
+from jax.experimental.pallas import tpu as pltpu
 from jax.sharding import Mesh
 from jax.sharding import PartitionSpec as P
 
 TM = ("chip", "core")
+MESH = pl.DeviceIdType.MESH
 
 
 def halo(block, width):
@@ -25,38 +28,88 @@
     return (kappa_cols[:, :, None] + 4.0) * centre - beside
 
 
+def gather_kernel(chol_ref, zero, out_ref, send_sems, recv_sems, local_sems):
+    G = out_ref.shape[0]
+    CH = out_ref.shape[1] // G
+    space = lax.axis_index("space")
+    core = lax.axis_index("core")
+    me = lax.axis_index("chip")
+    barrier = pltpu.get_barrier_semaphore()
+    for d in range(1, G):
+        pl.semaphore_signal(barrier, inc=1, device_id=(space, lax.rem(me + d, G), core), device_id_type=MESH)
+    pl.semaphore_wait(barrier, G - 1)
+
+    def chunk(i):
+        return pl.ds(pl.multiple_of((me + i) * CH, CH), CH)
+
+    def remote(d, i):
+        return pltpu.make_async_remote_copy(
+            src_ref=chol_ref.at[chunk(i)],
+            dst_ref=out_ref.at[me, chunk(i)],
+            send_sem=send_sems.at[d * G + i],
+            recv_sem=recv_sems.at[me * G + i],
+            device_id=(space, lax.rem(me + d, G), core),
+            device_id_type=MESH,
+        )
+
+    def own(i):
+        return pltpu.make_async_copy(chol_ref.at[chunk(i)], out_ref.at[me, chunk(i)], local_sems.at[i])
+
+    def blank(k, i):
+        return pltpu.make_async_copy(zero, out_ref.at[k, pl.ds(i * CH, CH)], local_sems.at[G + k * G + i])
+
+    for i in range(G):
+        @pl.when(me + i < G)
+        def _():
+            for d in range(1, G):
+                remote(d, i).start()
+    for i in range(G):
+        @pl.when(me + i < G)
+        def _():
+            own(i).start()
+    for k in range(G):
+        for i in range(k):
+            blank(k, i).start()
+    for k in range(G):
+        for i in range(k):
+            blank(k, i).wait()
+    for i in range(G):
+        @pl.when(me + i < G)
+        def _():
+            own(i).wait()
+            for d in range(1, G):
+                remote(d, i).wait_send()
+    for k in range(G):
+        for i in range(G - k):
+            @pl.when(me != k)
+            def _():
+                rows = pl.ds((k + i) * CH, CH)
+                pltpu.make_async_remote_copy(
+                    src_ref=chol_ref.at[rows],
+                    dst_ref=out_ref.at[k, rows],
+                    send_sem=send_sems.at[i],
+                    recv_sem=recv_sems.at[k * G + i],
+                    device_id=(space, k, core),
+                    device_id_type=MESH,
+                ).wait_recv()
+
+
 def gather_factor(chol_cols):
-    g = lax.axis_size("chip")
-    cores = lax.axis_size("core")
+    G = lax.axis_size("chip")
     T, B = chol_cols.shape
-    S = cores * B
-    H = (2 * T - (g - 1) * S) // 2
-    tail = T - H
-    k = lax.axis_index("chip")
-    pairs = [(i, g - 1 - i) for i in range(g // 2)]
-    sent = lax.ppermute(chol_cols[H:], "chip", pairs)
-    own_low = lax.dynamic_slice_in_dim(chol_cols, k * S, H, axis=0)
-    partner = g - 1 - k
-    length = T - partner * S - H
-    shifted = lax.dynamic_slice_in_dim(
-        jnp.concatenate([sent, jnp.zeros((H, B), sent.dtype)], axis=0), tail - length, H, axis=0
-    )
-    own_tail = chol_cols[T - H:]
-    rows = lax.broadcasted_iota(jnp.int32, (H, B), 0)
-    own_high = jnp.where(rows < length, shifted, own_tail)
-    piece = jnp.where(k < g // 2, own_low, own_high)
-    gathered = lax.all_gather(piece, "chip", axis=0, tiled=False)
-    blocks = []
-    for c in range(g):
-        p = g - 1 - c
-        if c < g // 2:
-            length_c = T - c * S - H
-            nonzero = jnp.concatenate([gathered[c], gathered[p, :length_c]], axis=0)
-        else:
-            length_p = T - p * S - H
-            nonzero = gathered[c, length_p:]
-        blocks.append(jnp.concatenate([jnp.zeros((c * S, B), nonzero.dtype), nonzero], axis=0))
-    return jnp.stack(blocks, axis=0)
+    CH = T // G
+    return pl.pallas_call(
+        gather_kernel,
+        out_shape=jax.ShapeDtypeStruct((G, T, B), chol_cols.dtype),
+        in_specs=[pl.BlockSpec(memory_space=pl.ANY)] * 2,
+        out_specs=pl.BlockSpec(memory_space=pl.ANY),
+        scratch_shapes=[
+            pltpu.SemaphoreType.DMA((G * G,)),
+            pltpu.SemaphoreType.DMA((G * G,)),
+            pltpu.SemaphoreType.DMA((G + G * G,)),
+        ],
+        compiler_params=pltpu.CompilerParams(collective_id=0, has_side_effects=True),
+    )(chol_cols, jnp.zeros((CH, B), chol_cols.dtype))
 
 
 def local(latent, events, log_base, innovation, kappa_sq, chol_factor, step_size):

time: 238 us -> 260 us (1.092)
  Pallas kernels: 0 us -> 148 us
  waiting for transfers between devices: 145 us -> 31 us
  local copies, waits for them, and re-layouts: 21 us -> 13 us
  starting transfers between devices: 15.6 us -> 11.9 us
  other arithmetic: 10 us -> 6.31 us
  matrix products: 15.5 us -> 18.8 us
    pallas_call x0 -> x1, Pallas kernels: none -> 148 us  [gather_factor(): pl.pallas_call(gather_kernel, out_shape=jax.ShapeDtypeStruct((G, T, B), c...]
    all_gather x1 -> x0, waiting for transfers between devices: 102 us -> none  [gather_factor(): gathered = lax.all_gather(piece, 'chip', axis=0, tiled=False)]
    squeeze x8 -> x0, local copies, waits for them, and re-layouts: 7.81 us -> none  [the longest x4 3.98 us: gather_factor(): nonzero = gathered[c, length_p:]]
    ppermute x1 -> x0, waiting for transfers between devices: 7.07 us -> none  [gather_factor(): sent = lax.ppermute(chol_cols[H:], 'chip', pairs)]
    all_gather x1, waiting for transfers between devices: 4.45 us -> 0.02 us  [local(): lax.all_gather(by_chip.reshape(group, g, time_count), 'core', axis=0, til...]
    ppermute x1 -> x0, starting transfers between devices: 3.71 us -> none  [gather_factor(): sent = lax.ppermute(chol_cols[H:], 'chip', pairs)]
    dot_general x1, matrix products: 5.58 us -> 9.02 us  [local(): lax.dot_general(hours, factor, (((1,), (1,)), ((), ())), precision=lax.Pr...]
  transfers between devices with their start and end apart: 7 -> 5, of which waited for: 6 -> 3; matrix products, arithmetic and copies ran while one was open for 3% -> 1% of each run, Pallas kernels for 0% -> 57%
where the time goes in v3:
time: 260 us; the launch traced here: 259 us
  Pallas kernels  148 us (57%)
  waiting for transfers between devices  31 us (12%)
  matrix products  18.8 us (7%)
  blocking collectives  15.1 us (6%)
  between operations  14.8 us (6%)
  local copies, waits for them, and re-layouts  13 us (5%)
  starting transfers between devices  11.9 us (5%)
  other arithmetic  6.31 us (2%)
    pallas_call x1, Pallas kernels, gather_factor(): pl.pallas_call(gather_kernel, out_shape=jax.ShapeDtypeStruct((G, T, B), c...  148 us
    all_to_all x1, blocking collectives, local(): by_chip = lax.all_to_all(flattened, 'chip', 0, 1, tiled=True)  15.1 us
    reduce_scatter x1, waiting for transfers between devices, local(): summed = lax.psum_scatter(split, 'core', scatter_dimension=0, tiled=True)[0]  14.8 us
    all_to_all x1, waiting for transfers between devices, local(): prior = lax.all_to_all(summed, 'chip', 1, 0, tiled=True)  11.8 us
    dot_general x1, matrix products, local(): lax.dot_general(projected, factor, (((1, 2), (0, 2)), ((), ())), precisio...  9.74 us
    dot_general x1, matrix products, local(): lax.dot_general(hours, factor, (((1,), (1,)), ((), ())), precision=lax.Pr...  9.02 us
    ppermute x1, starting transfers between devices, halo(): lax.ppermute(lax.slice_in_dim(block, cols - width, None, axis=1), 'space'...  5.73 us
  transfers between devices with their start and end apart: 5, of which 3 were waited for; matrix products, arithmetic and copies ran while one was open for 1% of the time, Pallas kernels for 57%

profile of v3, /device:TPU:1, one launch (start us, length us, event | category | flops | bytes accessed | tf_op | source)
XLA Modules:
  0.0 259.0 jit_solution(15916555803027077423)
XLA Ops:
  7.2 0.0 copy-start.1
  7.2 0.0 all-gather.3.cloned.1.call-start
  7.2 1.0 fusion.11
  8.3 5.7 %collective-permute-start = (f32[24,2,128]{2,1,0:T(2,128)S(1)}, f32[24,2,128]{2,1,0:T(2,128)S(1)}, u32[]{:S(2)}, u32[]{:S(2)}) collective-permute-start(f32[24,2,128]{2,1,0:T(2,128)S(1)} %get-tuple-element.4), channel_id=1, source_target_pairs={{0,16},{16,32},{32,48},{48,64},{64,80},{80,96},{96,112},{112,128},... | collective-permute-start | bytes 73736 | tf_op jit(solution)/shard_map/ppermute | solution.py:18
  14.0 1.3 collective-permute-start.1
  15.3 0.8 fusion.9
  16.1 0.8 fusion.10
  17.0 0.0 collective-permute-done
  17.0 4.3 %collective-permute-done.1 = f32[24,2,128]{2,1,0:T(2,128)S(1)} collective-permute-done((f32[24,2,128]{2,1,0:T(2,128)S(1)}, f32[24,2,128]{2,1,0:T(2,128)S(1)}, u32[]{:S(2)}, u32[]{:S(2)}) %collective-permute-start.1) | collective-permute-done | bytes 24608 | tf_op jit(solution)/shard_map/ppermute | solution.py:19
  21.3 1.2 pad_maximum_fusion
  22.5 0.0 copy-done.1
  22.5 0.4 fusion.4
  23.0 0.1 slice.48
  23.0 0.3 fusion.8
  23.4 15.1 %all_to_all.31 = f32[8,192,128]{2,1,0:T(8,128)} all-to-all(f32[8,192,128]{2,1,0:T(8,128)S(1)} %bitcast.25), channel_id=1, replica_groups=mesh['space'=16,'chip'=8,'core'=2] {'chip'}, dimensions={0} | all-to-all | bytes 1572864 | tf_op jit(solution)/shard_map/all_to_all | solution.py:135
  38.5 0.0 all-gather.3.cloned.1.call-update
  38.5 0.0 reduce-scatter.2.cloned.1.call-start
  38.6 0.7 broadcast_in_dim.19.zero
  39.2 148.1 %shard_map.86 = f32[8,2048,128]{2,1,0:T(8,128)} custom-call(f32[2048,128]{1,0:T(8,128)} %chol_ref.1, f32[256,128]{1,0:T(8,128)} %broadcast_in_dim.19.zero), custom_call_target="tpu_custom_call" | custom-call | tf_op jit(solution)/shard_map/pallas_call | solution.py:101
  187.3 0.0 all-gather.3.cloned.1.call-done
  187.4 2.6 %copy.17 = f32[192,8,2,128]{3,2,1,0:T(2,128)S(1)} copy(f32[192,8,2,128]{3,0,2,1:T(8,128)} %bitcast.27) | data formatting | bytes 3145728 | tf_op jit(solution)/shard_map/transpose | solution.py:137
  190.0 2.5 reshape.43
  192.5 0.0 copy-start
  192.5 9.0 %fusion.12 = f32[192,8,128]{2,0,1:T(8,128)S(1)} fusion(f32[192,2048,1]{1,0,2:T(8,128)} %reshape.43, f32[8,2048,128]{2,1,0:T(8,128)} %shard_map.86), kind=kOutput, calls=%fused_computation.25 | convolution fusion | flops 4831838208 | bytes 10747904 | tf_op jit(solution)/shard_map/dot_general | solution.py:138
  201.5 0.0 copy-done
  201.5 9.7 %convolution_bitcast_fusion = f32[192,2048]{1,0:T(8,128)} fusion(f32[192,8,128]{2,0,1:T(8,128)S(1)} %fusion.12, f32[8,2048,128]{2,1,0:T(8,128)S(1)} %copy-done), kind=kOutput, calls=%fused_computation | convolution fusion | flops 4831838208 | bytes 10747904 | tf_op jit(solution)/shard_map/dot_general | solution.py:142
  211.2 2.6 %reshape.40 = f32[192,8,2,128]{3,2,1,0:T(2,128)S(1)} reshape(f32[192,2048]{1,0:T(8,128)} %convolution_bitcast_fusion) | data formatting | bytes 3145728 | tf_op jit(solution)/shard_map/reshape | solution.py:146
  213.9 1.3 copy.22
  215.1 0.0 reduce-scatter.2.cloned.1.call-update
  215.2 14.8 %reduce-scatter.2.cloned.1.call-done = f32[1,192,8,128]{3,2,1,0:T(8,128)} async-done(((f32[2,192,8,128]{3,2,1,0:T(8,128)}), f32[1,192,8,128]{3,2,1,0:T(8,128)}) %reduce-scatter.2.cloned.1.call-update) | async-done | bytes 786448 | tf_op jit(solution)/shard_map/reduce_scatter | solution.py:147
  229.9 0.0 copy-start.2
  229.9 0.0 copy-start.3
  229.9 2.3 copy.19
  232.2 4.8 %all-to-all-start.1 = ((f32[192,8,128]{2,0,1:T(8,128)}), f32[192,8,128]{2,0,1:T(8,128)S(1)}, u32[]{:S(2)}, u32[]{:S(2)}) async-start(f32[192,8,128]{2,0,1:T(8,128)} %copy.19), calls=%async_computation.2 | async-start | bytes 1572864 | tf_op jit(solution)/shard_map/all_to_all | solution.py:148
  237.7 11.8 %all-to-all-done.1 = f32[192,8,128]{2,0,1:T(8,128)S(1)} async-done(((f32[192,8,128]{2,0,1:T(8,128)}), f32[192,8,128]{2,0,1:T(8,128)S(1)}, u32[]{:S(2)}, u32[]{:S(2)}) %all-to-all-start.1) | async-done | bytes 786464 | tf_op jit(solution)/shard_map/all_to_all | solution.py:148
  249.5 0.0 copy-done.2
  249.5 0.0 copy-done.3
  249.5 2.7 %multiply_add_fusion = (f32[24,64,128]{2,1,0:T(8,128)}, f32[24,64,128]{2,1,0:T(8,128)}) fusion(f32[24,64,128]{2,1,0:T(8,128)S(1)} %copy-done.2, f32[24,64,128]{2,1,0:T(8,128)S(1)} %copy-done.1, f32[]{:T(128)S(6)} %sqrt.3, f32[]{:T(128)} %bitcast.21, f32[24,64,128]{2,1,0:T(8,128)S(1)} %bitcast.26, f32[24,64,128]{2,1,0:T(8,128)S(1)} %copy-done.3, ...), kind=kLoop, calls=%fused_computation.17 | loop fusion | flops 1572864 | bytes 5505032 | tf_op jit(solution)/shard_map/add | solution.py:151
  (1 shorter events, 0.0 us)
Async XLA Ops:
  7.2 15.4 %copy-start.1 = (f32[24,64,128]{2,1,0:T(8,128)S(1)}, f32[24,64,128]{2,1,0:T(8,128)}, u32[]{:S(2)}) copy-start(f32[24,64,128]{2,1,0:T(8,128)} %param.7) | copy-start | bytes 2359300
  7.2 180.2 %all-gather.3.cloned.1.call-start = ((), (), s32[]{:S(2)}) async-start(), calls=%async_computation.4 | async-start | bytes 2359296 | tf_op jit(solution)/shard_map/all_gather | solution.py:136
  8.3 8.7 %collective-permute-start = (f32[24,2,128]{2,1,0:T(2,128)S(1)}, f32[24,2,128]{2,1,0:T(2,128)S(1)}, u32[]{:S(2)}, u32[]{:S(2)}) collective-permute-start(f32[24,2,128]{2,1,0:T(2,128)S(1)} %get-tuple-element.4), channel_id=1, source_target_pairs={{0,16},{16,32},{32,48},{48,64},{64,80},{80,96},{96,112},{112,128},... | collective-permute-start | bytes 73736 | tf_op jit(solution)/shard_map/ppermute | solution.py:18
  14.0 7.3 %collective-permute-start.1 = (f32[24,2,128]{2,1,0:T(2,128)S(1)}, f32[24,2,128]{2,1,0:T(2,128)S(1)}, u32[]{:S(2)}, u32[]{:S(2)}) collective-permute-start(f32[24,2,128]{2,1,0:T(2,128)S(1)} %get-tuple-element.5), channel_id=1, source_target_pairs={{16,0},{32,16},{48,32},{64,48},{80,64},{96,80},{112,96},{128,112},... | collective-permute-start | bytes 73736 | tf_op jit(solution)/shard_map/ppermute | solution.py:19
  38.5 191.4 %reduce-scatter.2.cloned.1.call-start = ((), (), s32[]{:S(2)}) async-start(), calls=%async_computation.3 | async-start | bytes 2359296 | tf_op jit(solution)/shard_map/reduce_scatter | solution.py:147
  192.5 9.0 %copy-start = (f32[8,2048,128]{2,1,0:T(8,128)S(1)}, f32[8,2048,128]{2,1,0:T(8,128)}, u32[]{:S(2)}) copy-start(f32[8,2048,128]{2,1,0:T(8,128)} %shard_map.86) | copy-start | bytes 25165828
  229.9 19.6 %copy-start.2 = (f32[24,64,128]{2,1,0:T(8,128)S(1)}, f32[24,64,128]{2,1,0:T(8,128)}, u32[]{:S(2)}) copy-start(f32[24,64,128]{2,1,0:T(8,128)} %param.10) | copy-start | bytes 2359300
  229.9 19.6 %copy-start.3 = (f32[24,64,128]{2,1,0:T(8,128)S(1)}, f32[24,64,128]{2,1,0:T(8,128)}, u32[]{:S(2)}) copy-start(f32[24,64,128]{2,1,0:T(8,128)} %param.9) | copy-start | bytes 2359300
  232.2 17.3 %all-to-all-start.1 = ((f32[192,8,128]{2,0,1:T(8,128)}), f32[192,8,128]{2,0,1:T(8,128)S(1)}, u32[]{:S(2)}, u32[]{:S(2)}) async-start(f32[192,8,128]{2,0,1:T(8,128)} %copy.19), calls=%async_computation.2 | async-start | bytes 1572864 | tf_op jit(solution)/shard_map/all_to_all | solution.py:148
Sparse Core Ops, SparseCore 0:
  38.6 16.3 all-gather.2
  215.3 14.5 reduce-scatter.1

commit v4 on v1

--- a/solution.py
+++ b/solution.py
@@ -1,6 +1,8 @@
 import jax
 import jax.numpy as jnp
 from jax import lax
+from jax.experimental import pallas as pl
+from jax.experimental.pallas import tpu as pltpu
 from jax.sharding import PartitionSpec as P
 
 
@@ -22,10 +24,14 @@
     return (kappa_cols[:, :, None] + 4.0) * centre - beside
 
 
+def fold_rows(T, B, n):
+    return -(-(T + B) // (2 * B)) * B
+
+
 def gather_factor(chol_cols):
     n = lax.axis_size("tm")
     T, B = chol_cols.shape
-    H = (n + 1) * B // 2
+    H = fold_rows(T, B, n)
     tail = T - H
     j = lax.axis_index("tm")
     pairs = [(i, n - 1 - i) for i in range(n // 2)]
@@ -40,19 +46,57 @@
     rows = lax.broadcasted_iota(jnp.int32, (H, B), 0)
     own_high = jnp.where(rows < length, shifted, own_tail)
     piece = jnp.where(j < n // 2, own_low, own_high)
-    gathered = lax.all_gather(piece, "tm", axis=0, tiled=False)
-    blocks = []
+    return lax.all_gather(piece, "tm", axis=0, tiled=False)
+
+
+def segments(n, T, B, H):
+    out = []
     for c in range(n):
+        p = n - 1 - c
         if c < n // 2:
-            p = n - 1 - c
-            length_c = (n - c) * B - H
-            nonzero = jnp.concatenate([gathered[c], gathered[p, :length_c]], axis=0)
+            segs = [(c, 0, c * B, H)]
+            if T - c * B - H > 0:
+                segs.append((p, 0, c * B + H, T - c * B - H))
         else:
-            p = n - 1 - c
-            length_p = (n - p) * B - H
-            nonzero = gathered[c, length_p:]
-        blocks.append(jnp.concatenate([jnp.zeros((c * B, B), nonzero.dtype), nonzero], axis=0))
-    return jnp.concatenate(blocks, axis=1)
+            segs = [(c, H - (T - c * B), c * B, T - c * B)]
+        out.append(segs)
+    return out
+
+
+def prior_kernel(s_ref, g_ref, out_ref):
+    n, H, B = g_ref.shape
+    N, T = s_ref.shape
+    out_ref[...] = jnp.zeros_like(out_ref)
+    for segs in segments(n, T, B, H):
+        proj = None
+        for slot, r0, h0, count in segs:
+            term = jnp.dot(
+                s_ref[:, h0:h0 + count], g_ref[slot, r0:r0 + count, :],
+                precision=lax.Precision.HIGHEST, preferred_element_type=jnp.float32,
+            )
+            proj = term if proj is None else proj + term
+        for slot, r0, h0, count in segs:
+            out_ref[:, h0:h0 + count] += lax.dot_general(
+                proj, g_ref[slot, r0:r0 + count, :], (((1,), (1,)), ((), ())),
+                precision=lax.Precision.HIGHEST, preferred_element_type=jnp.float32,
+            )
+
+
+def prior_of(by_cell, gathered):
+    n, H, B = gathered.shape
+    N, T = by_cell.shape
+    flops = 0
+    for segs in segments(n, T, B, H):
+        flops += sum(4 * N * count * B for _, _, _, count in segs)
+    return pl.pallas_call(
+        prior_kernel,
+        out_shape=jax.ShapeDtypeStruct((N, T), jnp.float32),
+        in_specs=[pl.BlockSpec(memory_space=pltpu.VMEM)] * 2,
+        out_specs=pl.BlockSpec(memory_space=pltpu.VMEM),
+        cost_estimate=pl.CostEstimate(
+            flops=flops, transcendentals=0, bytes_accessed=4 * (2 * N * T + n * H * B)
+        ),
+    )(by_cell, gathered)
 
 
 def local(latent, events, log_base, innovation, kappa_sq, chol_factor, step_size):
@@ -63,7 +107,7 @@
     kappa_wide = lax.dynamic_slice(
         padded_kappa, (jnp.int32(0), col_index * col_count), (row_count, col_count + 2)
     )
-    full = gather_factor(chol_factor)
+    gathered = gather_factor(chol_factor)
     extended = halo(latent, 2)
     first_pass = operate(extended, kappa_wide)
     cols = lax.broadcasted_iota(jnp.int32, (1, col_count + 2, 1), 1)
@@ -73,16 +117,7 @@
     cell_count = row_count * col_count
     flattened = spatial.reshape(cell_count, time_count)
     by_cell = lax.all_to_all(flattened, "tm", 0, 1, tiled=True)
-    projected = jnp.dot(
-        by_cell, full, precision=lax.Precision.HIGHEST, preferred_element_type=jnp.float32
-    )
-    prior_cells = lax.dot_general(
-        projected,
-        full,
-        (((1,), (1,)), ((), ())),
-        precision=lax.Precision.HIGHEST,
-        preferred_element_type=jnp.float32,
-    )
+    prior_cells = prior_of(by_cell, gathered)
     prior = lax.all_to_all(prior_cells, "tm", 1, 0, tiled=True)
     prior_term = prior.reshape(row_count, col_count, time_count)
     gradient = events.astype(jnp.float32) - jnp.exp(log_base + latent) - prior_term

time: 199 us -> 153 us (0.77)
  matrix products: 33.3 us -> 0 us
  blocking collectives: 0 us -> 28.9 us
  local copies, waits for them, and re-layouts: 29.8 us -> 5.16 us
  Pallas kernels: 0 us -> 23 us
  waiting for transfers between devices: 71.3 us -> 51.9 us
  other arithmetic: 21.5 us -> 9.93 us
  starting transfers between devices: 26.5 us -> 18.8 us
    dot_general x2 -> x0, matrix products: 33.3 us -> none  [the longest x1 19.8 us: local(): lax.dot_general(projected, full, (((1,), (1,)), ((), ())), precision=lax....]
    all_to_all x0 -> x1, blocking collectives: none -> 28.9 us  [local(): by_cell = lax.all_to_all(flattened, 'tm', 0, 1, tiled=True)]
    pallas_call x0 -> x1, Pallas kernels: none -> 23 us  [prior_of(): pl.pallas_call(prior_kernel, out_shape=jax.ShapeDtypeStruct((N, T), jnp.f...]
    all_gather x1, waiting for transfers between devices: 44.7 us -> 25.9 us  [gather_factor(): return lax.all_gather(piece, 'tm', axis=0, tiled=False)]
    squeeze x16 -> x0, local copies, waits for them, and re-layouts: 15.4 us -> none  [the longest x8 7.81 us: gather_factor(): nonzero = gathered[c, length_p:]]
    unnamed x8 -> x0, other arithmetic: 10.7 us -> none
    all_to_all x1 -> x0, starting transfers between devices: 7.71 us -> none  [local(): by_cell = lax.all_to_all(flattened, 'tm', 0, 1, tiled=True)]
    unnamed x13 -> x6, local copies, waits for them, and re-layouts: 7.64 us -> 0.02 us
  transfers between devices with their start and end apart: 6 -> 5, of which waited for: 4 -> 4; matrix products, arithmetic and copies ran while one was open for 22% -> 5% of each run, Pallas kernels for 0% -> 0%
where the time goes in v4:
time: 153 us; the launch traced here: 152 us
  waiting for transfers between devices  51.9 us (34%)
  blocking collectives  28.9 us (19%)
  Pallas kernels  23 us (15%)
  starting transfers between devices  18.8 us (12%)
  between operations  14.8 us (10%)
  other arithmetic  9.93 us (6%)
  local copies, waits for them, and re-layouts  5.16 us (3%)
    all_to_all x1, blocking collectives, local(): by_cell = lax.all_to_all(flattened, 'tm', 0, 1, tiled=True)  28.9 us
    all_gather x1, waiting for transfers between devices, gather_factor(): return lax.all_gather(piece, 'tm', axis=0, tiled=False)  25.9 us
    pallas_call x1, Pallas kernels, prior_of(): pl.pallas_call(prior_kernel, out_shape=jax.ShapeDtypeStruct((N, T), jnp.f...  23 us
    all_to_all x1, waiting for transfers between devices, local(): prior = lax.all_to_all(prior_cells, 'tm', 1, 0, tiled=True)  12.3 us
    ppermute x1, waiting for transfers between devices, gather_factor(): sent = lax.ppermute(chol_cols[T - tail:], 'tm', pairs)  10.3 us
    ppermute x1, starting transfers between devices, gather_factor(): sent = lax.ppermute(chol_cols[T - tail:], 'tm', pairs)  7.41 us
    all_to_all x1, starting transfers between devices, local(): prior = lax.all_to_all(prior_cells, 'tm', 1, 0, tiled=True)  5.18 us
    ppermute x1, starting transfers between devices, halo(): lax.ppermute(lax.slice_in_dim(block, cols - width, None, axis=1), 'space'...  4.9 us
  transfers between devices with their start and end apart: 5, of which 4 were waited for; matrix products, arithmetic and copies ran while one was open for 5% of the time, Pallas kernels for 0%

profile of v4, /device:TPU:1, one launch (start us, length us, event | category | flops | bytes accessed | tf_op | source)
XLA Modules:
  0.0 152.4 jit_solution(10921452304193891122)
XLA Ops:
  7.2 0.0 all-gather.3.cloned.1.call-start
  7.2 1.1 slice.54
  8.3 7.4 %collective-permute-start.2 = (f32[896,128]{1,0:T(8,128)S(1)}, f32[896,128]{1,0:T(8,128)S(1)}, u32[]{:S(2)}, u32[]{:S(2)}) collective-permute-start(f32[896,128]{1,0:T(8,128)S(1)} %slice.54), channel_id=1, source_target_pairs={{0,15},{1,14},{2,13},{3,12},{4,11},{5,10},{6,9},{7,8},{16,31},{17,... | collective-permute-start | bytes 1376264 | tf_op jit(solution)/shard_map/ppermute | solution.py:38
  15.7 10.3 %collective-permute-done.2 = f32[896,128]{1,0:T(8,128)S(1)} collective-permute-done((f32[896,128]{1,0:T(8,128)S(1)}, f32[896,128]{1,0:T(8,128)S(1)}, u32[]{:S(2)}, u32[]{:S(2)}) %collective-permute-start.2) | collective-permute-done | bytes 458784 | tf_op jit(solution)/shard_map/ppermute | solution.py:38
  26.0 2.3 %fusion.10 = f32[1152,128]{1,0:T(8,128)} fusion(s32[]{:T(128)S(6)} %select_n.29, f32[896,128]{1,0:T(8,128)S(1)} %collective-permute-done.2, f32[2048,128]{1,0:T(8,128)} %param.12, s32[]{:T(128)S(6)} %select_n.28, pred[1152]{0:T(1024)(128)(4,1)S(1)} %iota_compare_fusion, pred[]{:T(512)S(6)} %lt.20), kind=kLoop, calls=%fused_computation.21 | loop fusion | flops 294912 | bytes 2229385 | tf_op jit(solution)/shard_map/jit(_where)/select_n | solution.py:48
  28.3 0.0 all-gather.3.cloned.1.call-update
  28.3 1.0 fusion.13
  29.3 4.9 %collective-permute-start = (f32[24,2,128]{2,1,0:T(2,128)S(1)}, f32[24,2,128]{2,1,0:T(2,128)S(1)}, u32[]{:S(2)}, u32[]{:S(2)}) collective-permute-start(f32[24,2,128]{2,1,0:T(2,128)S(1)} %get-tuple-element.4), channel_id=1, source_target_pairs={{0,16},{16,32},{32,48},{48,64},{64,80},{80,96},{96,112},{112,128},... | collective-permute-start | bytes 73736 | tf_op jit(solution)/shard_map/ppermute | solution.py:14
  34.2 1.3 collective-permute-start.1
  35.5 0.8 fusion.11
  36.3 0.8 fusion.12
  37.1 0.0 collective-permute-done
  37.1 3.4 %collective-permute-done.1 = f32[24,2,128]{2,1,0:T(2,128)S(1)} collective-permute-done((f32[24,2,128]{2,1,0:T(2,128)S(1)}, f32[24,2,128]{2,1,0:T(2,128)S(1)}, u32[]{:S(2)}, u32[]{:S(2)}) %collective-permute-start.1) | collective-permute-done | bytes 24608 | tf_op jit(solution)/shard_map/ppermute | solution.py:15
  40.6 1.2 pad_maximum_fusion
  41.8 1.7 %fusion.4 = f32[24,66,128]{2,1,0:T(8,128)S(1)} fusion(f32[24,66,128]{2,1,0:T(8,128)S(1)} %pad_maximum_fusion, f32[24,2,128]{2,1,0:T(2,128)S(1)} %collective-permute-done.1, f32[24,64,128]{2,1,0:T(8,128)} %param.7, f32[24,2,128]{2,1,0:T(2,128)S(1)} %collective-permute-done, f32[24,66]{1,0:T(8,128)S(1)} %fusion.11, pred[66]{0:T(512)(128)(4,1)S(1)} %and_or_fusion), kind=kLoop, calls=%fused_computation.7 | loop fusion | flops 1622016 | bytes 2464002 | tf_op jit(solution)/shard_map/jit(_where)/select_n | solution.py:115
  43.5 0.1 slice.56
  43.6 0.3 fusion.8
  43.9 0.0 copy-start
  44.0 0.0 copy-start.1
  44.0 0.0 copy-start.2
  44.0 28.9 %all_to_all.35 = f32[16,96,128]{2,1,0:T(8,128)S(1)} all-to-all(f32[16,96,128]{2,1,0:T(8,128)S(1)} %bitcast.20), channel_id=1, replica_groups=mesh['space'=16,'tm'=16] {'tm'}, dimensions={0} | all-to-all | bytes 1572864 | tf_op jit(solution)/shard_map/all_to_all | solution.py:119
  72.9 0.9 copy_bitcast_fusion.s_ref
  73.8 25.9 %all-gather.3.cloned.1.call-done = f32[18432,128]{1,0:T(8,128)} async-done(((f32[1152,128]{1,0:T(8,128)}), f32[18432,128]{1,0:T(8,128)}) %all-gather.3.cloned.1.call-update) | async-done | bytes 9437200 | tf_op jit(solution)/shard_map/all_gather | solution.py:49
  99.7 23.0 %shard_map.86 = f32[96,2048]{1,0:T(8,128)} custom-call(f32[96,2048]{1,0:T(8,128)} %copy_bitcast_fusion.s_ref, f32[16,1152,128]{2,1,0:T(8,128)} %bitcast.19), custom_call_target="tpu_custom_call" | custom-call | flops 855638016 | bytes 11010048 | tf_op jit(solution)/shard_map/pallas_call | solution.py:91
  122.6 2.1 %copy_bitcast_fusion.1 = f32[96,16,128]{2,0,1:T(8,128)} fusion(f32[96,2048]{1,0:T(8,128)} %shard_map.86), kind=kLoop, calls=%fused_computation.17 | loop fusion | bytes 1572864 | tf_op jit(solution)/shard_map/all_to_all | solution.py:121
  124.7 5.2 %all-to-all-start.1 = ((f32[96,16,128]{2,0,1:T(8,128)}), f32[96,16,128]{2,0,1:T(8,128)S(1)}, u32[]{:S(2)}, u32[]{:S(2)}) async-start(f32[96,16,128]{2,0,1:T(8,128)} %copy_bitcast_fusion.1), calls=%async_computation.1 | async-start | bytes 1572864 | tf_op jit(solution)/shard_map/all_to_all | solution.py:121
  130.6 12.3 %all-to-all-done.1 = f32[96,16,128]{2,0,1:T(8,128)S(1)} async-done(((f32[96,16,128]{2,0,1:T(8,128)}), f32[96,16,128]{2,0,1:T(8,128)S(1)}, u32[]{:S(2)}, u32[]{:S(2)}) %all-to-all-start.1) | async-done | bytes 786464 | tf_op jit(solution)/shard_map/all_to_all | solution.py:121
  142.9 0.0 copy-done
  142.9 0.0 copy-done.1
  142.9 0.0 copy-done.2
  142.9 2.7 %multiply_add_fusion = (f32[24,64,128]{2,1,0:T(8,128)}, f32[24,64,128]{2,1,0:T(8,128)}) fusion(f32[24,64,128]{2,1,0:T(8,128)S(1)} %copy-done.1, f32[24,64,128]{2,1,0:T(8,128)S(1)} %copy-done, f32[]{:T(128)S(6)} %sqrt.3, f32[]{:T(128)} %bitcast.17, f32[24,64,128]{2,1,0:T(8,128)S(1)} %bitcast.21, f32[24,64,128]{2,1,0:T(8,128)S(1)} %copy-done.2, ...), kind=kLoop, calls=%fused_computation.18 | loop fusion | flops 1572864 | bytes 5505032 | tf_op jit(solution)/shard_map/add | solution.py:124
  (2 shorter events, 0.0 us)
Async XLA Ops:
  7.2 92.5 %all-gather.3.cloned.1.call-start = ((), (), s32[]{:S(2)}) async-start(), calls=%async_computation.2 | async-start | bytes 10027008 | tf_op jit(solution)/shard_map/all_gather | solution.py:49
  8.3 17.7 %collective-permute-start.2 = (f32[896,128]{1,0:T(8,128)S(1)}, f32[896,128]{1,0:T(8,128)S(1)}, u32[]{:S(2)}, u32[]{:S(2)}) collective-permute-start(f32[896,128]{1,0:T(8,128)S(1)} %slice.54), channel_id=1, source_target_pairs={{0,15},{1,14},{2,13},{3,12},{4,11},{5,10},{6,9},{7,8},{16,31},{17,... | collective-permute-start | bytes 1376264 | tf_op jit(solution)/shard_map/ppermute | solution.py:38
  29.3 7.9 %collective-permute-start = (f32[24,2,128]{2,1,0:T(2,128)S(1)}, f32[24,2,128]{2,1,0:T(2,128)S(1)}, u32[]{:S(2)}, u32[]{:S(2)}) collective-permute-start(f32[24,2,128]{2,1,0:T(2,128)S(1)} %get-tuple-element.4), channel_id=1, source_target_pairs={{0,16},{16,32},{32,48},{48,64},{64,80},{80,96},{96,112},{112,128},... | collective-permute-start | bytes 73736 | tf_op jit(solution)/shard_map/ppermute | solution.py:14
  34.2 6.4 %collective-permute-start.1 = (f32[24,2,128]{2,1,0:T(2,128)S(1)}, f32[24,2,128]{2,1,0:T(2,128)S(1)}, u32[]{:S(2)}, u32[]{:S(2)}) collective-permute-start(f32[24,2,128]{2,1,0:T(2,128)S(1)} %get-tuple-element.5), channel_id=1, source_target_pairs={{16,0},{32,16},{48,32},{64,48},{80,64},{96,80},{112,96},{128,112},... | collective-permute-start | bytes 73736 | tf_op jit(solution)/shard_map/ppermute | solution.py:15
  43.9 98.9 %copy-start = (f32[24,64,128]{2,1,0:T(8,128)S(1)}, f32[24,64,128]{2,1,0:T(8,128)}, u32[]{:S(2)}) copy-start(f32[24,64,128]{2,1,0:T(8,128)} %param.7) | copy-start | bytes 2359300
  44.0 98.9 %copy-start.1 = (f32[24,64,128]{2,1,0:T(8,128)S(1)}, f32[24,64,128]{2,1,0:T(8,128)}, u32[]{:S(2)}) copy-start(f32[24,64,128]{2,1,0:T(8,128)} %param.10) | copy-start | bytes 2359300
  44.0 98.9 %copy-start.2 = (f32[24,64,128]{2,1,0:T(8,128)S(1)}, f32[24,64,128]{2,1,0:T(8,128)}, u32[]{:S(2)}) copy-start(f32[24,64,128]{2,1,0:T(8,128)} %param.9) | copy-start | bytes 2359300
  124.7 18.2 %all-to-all-start.1 = ((f32[96,16,128]{2,0,1:T(8,128)}), f32[96,16,128]{2,0,1:T(8,128)S(1)}, u32[]{:S(2)}, u32[]{:S(2)}) async-start(f32[96,16,128]{2,0,1:T(8,128)} %copy_bitcast_fusion.1), calls=%async_computation.1 | async-start | bytes 1572864 | tf_op jit(solution)/shard_map/all_to_all | solution.py:121
Sparse Core Ops, SparseCore 0:
  28.4 71.2 all-gather.2

commit v5 on v4

--- a/solution.py
+++ b/solution.py
@@ -72,13 +72,13 @@
         for slot, r0, h0, count in segs:
             term = jnp.dot(
                 s_ref[:, h0:h0 + count], g_ref[slot, r0:r0 + count, :],
-                precision=lax.Precision.HIGHEST, preferred_element_type=jnp.float32,
+                precision=lax.Precision.HIGH, preferred_element_type=jnp.float32,
             )
             proj = term if proj is None else proj + term
         for slot, r0, h0, count in segs:
             out_ref[:, h0:h0 + count] += lax.dot_general(
                 proj, g_ref[slot, r0:r0 + count, :], (((1,), (1,)), ((), ())),
-                precision=lax.Precision.HIGHEST, preferred_element_type=jnp.float32,
+                precision=lax.Precision.HIGH, preferred_element_type=jnp.float32,
             )
 
 

time: 153 us -> 144 us (0.941)
  Pallas kernels: 23 us -> 14.2 us
    pallas_call x1, Pallas kernels: 23 us -> 14.2 us  [prior_of(): pl.pallas_call(prior_kernel, out_shape=jax.ShapeDtypeStruct((N, T), jnp.f...]
where the time goes in v5:
time: 144 us
  waiting for transfers between devices  51.8 us (36%)
  blocking collectives  28.9 us (20%)
  starting transfers between devices  18.8 us (13%)
  between operations  14.8 us (10%)
  Pallas kernels  14.2 us (10%)
  other arithmetic  9.95 us (7%)
  local copies, waits for them, and re-layouts  5.16 us (4%)
    all_to_all x1, blocking collectives, local(): by_cell = lax.all_to_all(flattened, 'tm', 0, 1, tiled=True)  28.9 us
    all_gather x1, waiting for transfers between devices, gather_factor(): return lax.all_gather(piece, 'tm', axis=0, tiled=False)  25.8 us
    pallas_call x1, Pallas kernels, prior_of(): pl.pallas_call(prior_kernel, out_shape=jax.ShapeDtypeStruct((N, T), jnp.f...  14.2 us
    all_to_all x1, waiting for transfers between devices, local(): prior = lax.all_to_all(prior_cells, 'tm', 1, 0, tiled=True)  12.3 us
    ppermute x1, waiting for transfers between devices, gather_factor(): sent = lax.ppermute(chol_cols[T - tail:], 'tm', pairs)  10.3 us
    ppermute x1, starting transfers between devices, gather_factor(): sent = lax.ppermute(chol_cols[T - tail:], 'tm', pairs)  7.41 us
    all_to_all x1, starting transfers between devices, local(): prior = lax.all_to_all(prior_cells, 'tm', 1, 0, tiled=True)  5.19 us
    ppermute x1, starting transfers between devices, halo(): lax.ppermute(lax.slice_in_dim(block, cols - width, None, axis=1), 'space'...  4.9 us
  transfers between devices with their start and end apart: 5, of which 4 were waited for; matrix products, arithmetic and copies ran while one was open for 5% of the time, Pallas kernels for 0%

profile of v5, /device:TPU:1, one launch (start us, length us, event | category | flops | bytes accessed | tf_op | source)
XLA Modules:
  0.0 143.7 jit_solution(4759678587869161789)
XLA Ops:
  7.2 0.0 all-gather.3.cloned.1.call-start
  7.2 1.1 slice.54
  8.3 7.4 %collective-permute-start.2 = (f32[896,128]{1,0:T(8,128)S(1)}, f32[896,128]{1,0:T(8,128)S(1)}, u32[]{:S(2)}, u32[]{:S(2)}) collective-permute-start(f32[896,128]{1,0:T(8,128)S(1)} %slice.54), channel_id=1, source_target_pairs={{0,15},{1,14},{2,13},{3,12},{4,11},{5,10},{6,9},{7,8},{16,31},{17,... | collective-permute-start | bytes 1376264 | tf_op jit(solution)/shard_map/ppermute | solution.py:38
  15.7 10.3 %collective-permute-done.2 = f32[896,128]{1,0:T(8,128)S(1)} collective-permute-done((f32[896,128]{1,0:T(8,128)S(1)}, f32[896,128]{1,0:T(8,128)S(1)}, u32[]{:S(2)}, u32[]{:S(2)}) %collective-permute-start.2) | collective-permute-done | bytes 458784 | tf_op jit(solution)/shard_map/ppermute | solution.py:38
  26.0 2.3 %fusion.10 = f32[1152,128]{1,0:T(8,128)} fusion(s32[]{:T(128)S(6)} %select_n.29, f32[896,128]{1,0:T(8,128)S(1)} %collective-permute-done.2, f32[2048,128]{1,0:T(8,128)} %param.12, s32[]{:T(128)S(6)} %select_n.28, pred[1152]{0:T(1024)(128)(4,1)S(1)} %iota_compare_fusion, pred[]{:T(512)S(6)} %lt.20), kind=kLoop, calls=%fused_computation.21 | loop fusion | flops 294912 | bytes 2229385 | tf_op jit(solution)/shard_map/jit(_where)/select_n | solution.py:48
  28.3 0.0 all-gather.3.cloned.1.call-update
  28.3 1.0 fusion.13
  29.3 4.9 %collective-permute-start = (f32[24,2,128]{2,1,0:T(2,128)S(1)}, f32[24,2,128]{2,1,0:T(2,128)S(1)}, u32[]{:S(2)}, u32[]{:S(2)}) collective-permute-start(f32[24,2,128]{2,1,0:T(2,128)S(1)} %get-tuple-element.4), channel_id=1, source_target_pairs={{0,16},{16,32},{32,48},{48,64},{64,80},{80,96},{96,112},{112,128},... | collective-permute-start | bytes 73736 | tf_op jit(solution)/shard_map/ppermute | solution.py:14
  34.2 1.3 collective-permute-start.1
  35.5 0.8 fusion.11
  36.3 0.8 fusion.12
  37.1 0.0 collective-permute-done
  37.1 3.4 %collective-permute-done.1 = f32[24,2,128]{2,1,0:T(2,128)S(1)} collective-permute-done((f32[24,2,128]{2,1,0:T(2,128)S(1)}, f32[24,2,128]{2,1,0:T(2,128)S(1)}, u32[]{:S(2)}, u32[]{:S(2)}) %collective-permute-start.1) | collective-permute-done | bytes 24608 | tf_op jit(solution)/shard_map/ppermute | solution.py:15
  40.6 1.2 pad_maximum_fusion
  41.8 1.7 %fusion.4 = f32[24,66,128]{2,1,0:T(8,128)S(1)} fusion(f32[24,66,128]{2,1,0:T(8,128)S(1)} %pad_maximum_fusion, f32[24,2,128]{2,1,0:T(2,128)S(1)} %collective-permute-done.1, f32[24,64,128]{2,1,0:T(8,128)} %param.7, f32[24,2,128]{2,1,0:T(2,128)S(1)} %collective-permute-done, f32[24,66]{1,0:T(8,128)S(1)} %fusion.11, pred[66]{0:T(512)(128)(4,1)S(1)} %and_or_fusion), kind=kLoop, calls=%fused_computation.7 | loop fusion | flops 1622016 | bytes 2464002 | tf_op jit(solution)/shard_map/jit(_where)/select_n | solution.py:115
  43.6 0.1 slice.56
  43.6 0.3 fusion.8
  44.0 0.0 copy-start
  44.0 0.0 copy-start.1
  44.0 0.0 copy-start.2
  44.0 28.9 %all_to_all.35 = f32[16,96,128]{2,1,0:T(8,128)S(1)} all-to-all(f32[16,96,128]{2,1,0:T(8,128)S(1)} %bitcast.20), channel_id=1, replica_groups=mesh['space'=16,'tm'=16] {'tm'}, dimensions={0} | all-to-all | bytes 1572864 | tf_op jit(solution)/shard_map/all_to_all | solution.py:119
  72.9 0.9 copy_bitcast_fusion.s_ref
  73.8 25.8 %all-gather.3.cloned.1.call-done = f32[18432,128]{1,0:T(8,128)} async-done(((f32[1152,128]{1,0:T(8,128)}), f32[18432,128]{1,0:T(8,128)}) %all-gather.3.cloned.1.call-update) | async-done | bytes 9437200 | tf_op jit(solution)/shard_map/all_gather | solution.py:49
  99.7 14.2 %shard_map.86 = f32[96,2048]{1,0:T(8,128)} custom-call(f32[96,2048]{1,0:T(8,128)} %copy_bitcast_fusion.s_ref, f32[16,1152,128]{2,1,0:T(8,128)} %bitcast.19), custom_call_target="tpu_custom_call" | custom-call | flops 855638016 | bytes 11010048 | tf_op jit(solution)/shard_map/pallas_call | solution.py:91
  113.9 2.1 %copy_bitcast_fusion.1 = f32[96,16,128]{2,0,1:T(8,128)} fusion(f32[96,2048]{1,0:T(8,128)} %shard_map.86), kind=kLoop, calls=%fused_computation.17 | loop fusion | bytes 1572864 | tf_op jit(solution)/shard_map/all_to_all | solution.py:121
  116.0 5.2 %all-to-all-start.1 = ((f32[96,16,128]{2,0,1:T(8,128)}), f32[96,16,128]{2,0,1:T(8,128)S(1)}, u32[]{:S(2)}, u32[]{:S(2)}) async-start(f32[96,16,128]{2,0,1:T(8,128)} %copy_bitcast_fusion.1), calls=%async_computation.1 | async-start | bytes 1572864 | tf_op jit(solution)/shard_map/all_to_all | solution.py:121
  121.8 12.3 %all-to-all-done.1 = f32[96,16,128]{2,0,1:T(8,128)S(1)} async-done(((f32[96,16,128]{2,0,1:T(8,128)}), f32[96,16,128]{2,0,1:T(8,128)S(1)}, u32[]{:S(2)}, u32[]{:S(2)}) %all-to-all-start.1) | async-done | bytes 786464 | tf_op jit(solution)/shard_map/all_to_all | solution.py:121
  134.1 0.0 copy-done
  134.1 0.0 copy-done.1
  134.1 0.0 copy-done.2
  134.1 2.7 %multiply_add_fusion = (f32[24,64,128]{2,1,0:T(8,128)}, f32[24,64,128]{2,1,0:T(8,128)}) fusion(f32[24,64,128]{2,1,0:T(8,128)S(1)} %copy-done.1, f32[24,64,128]{2,1,0:T(8,128)S(1)} %copy-done, f32[]{:T(128)S(6)} %sqrt.3, f32[]{:T(128)} %bitcast.17, f32[24,64,128]{2,1,0:T(8,128)S(1)} %bitcast.21, f32[24,64,128]{2,1,0:T(8,128)S(1)} %copy-done.2, ...), kind=kLoop, calls=%fused_computation.18 | loop fusion | flops 1572864 | bytes 5505032 | tf_op jit(solution)/shard_map/add | solution.py:124
  (2 shorter events, 0.0 us)
Async XLA Ops:
  7.2 92.5 %all-gather.3.cloned.1.call-start = ((), (), s32[]{:S(2)}) async-start(), calls=%async_computation.2 | async-start | bytes 10027008 | tf_op jit(solution)/shard_map/all_gather | solution.py:49
  8.3 17.7 %collective-permute-start.2 = (f32[896,128]{1,0:T(8,128)S(1)}, f32[896,128]{1,0:T(8,128)S(1)}, u32[]{:S(2)}, u32[]{:S(2)}) collective-permute-start(f32[896,128]{1,0:T(8,128)S(1)} %slice.54), channel_id=1, source_target_pairs={{0,15},{1,14},{2,13},{3,12},{4,11},{5,10},{6,9},{7,8},{16,31},{17,... | collective-permute-start | bytes 1376264 | tf_op jit(solution)/shard_map/ppermute | solution.py:38
  29.3 7.9 %collective-permute-start = (f32[24,2,128]{2,1,0:T(2,128)S(1)}, f32[24,2,128]{2,1,0:T(2,128)S(1)}, u32[]{:S(2)}, u32[]{:S(2)}) collective-permute-start(f32[24,2,128]{2,1,0:T(2,128)S(1)} %get-tuple-element.4), channel_id=1, source_target_pairs={{0,16},{16,32},{32,48},{48,64},{64,80},{80,96},{96,112},{112,128},... | collective-permute-start | bytes 73736 | tf_op jit(solution)/shard_map/ppermute | solution.py:14
  34.2 6.4 %collective-permute-start.1 = (f32[24,2,128]{2,1,0:T(2,128)S(1)}, f32[24,2,128]{2,1,0:T(2,128)S(1)}, u32[]{:S(2)}, u32[]{:S(2)}) collective-permute-start(f32[24,2,128]{2,1,0:T(2,128)S(1)} %get-tuple-element.5), channel_id=1, source_target_pairs={{16,0},{32,16},{48,32},{64,48},{80,64},{96,80},{112,96},{128,112},... | collective-permute-start | bytes 73736 | tf_op jit(solution)/shard_map/ppermute | solution.py:15
  44.0 90.2 %copy-start = (f32[24,64,128]{2,1,0:T(8,128)S(1)}, f32[24,64,128]{2,1,0:T(8,128)}, u32[]{:S(2)}) copy-start(f32[24,64,128]{2,1,0:T(8,128)} %param.7) | copy-start | bytes 2359300
  44.0 90.2 %copy-start.1 = (f32[24,64,128]{2,1,0:T(8,128)S(1)}, f32[24,64,128]{2,1,0:T(8,128)}, u32[]{:S(2)}) copy-start(f32[24,64,128]{2,1,0:T(8,128)} %param.10) | copy-start | bytes 2359300
  44.0 90.2 %copy-start.2 = (f32[24,64,128]{2,1,0:T(8,128)S(1)}, f32[24,64,128]{2,1,0:T(8,128)}, u32[]{:S(2)}) copy-start(f32[24,64,128]{2,1,0:T(8,128)} %param.9) | copy-start | bytes 2359300
  116.0 18.2 %all-to-all-start.1 = ((f32[96,16,128]{2,0,1:T(8,128)}), f32[96,16,128]{2,0,1:T(8,128)S(1)}, u32[]{:S(2)}, u32[]{:S(2)}) async-start(f32[96,16,128]{2,0,1:T(8,128)} %copy_bitcast_fusion.1), calls=%async_computation.1 | async-start | bytes 1572864 | tf_op jit(solution)/shard_map/all_to_all | solution.py:121
Sparse Core Ops, SparseCore 0:
  28.4 71.2 all-gather.2
